TPU v7x, 512 devices: a whole 4x4x16 slice. The times are simulated.
512 devices in a mesh: roll: 64 (over x, z_hi, y, core), kv: 8 (over z_lo).
Axes of the slice: x: 4, y: 4, z: 16 (z_hi: 2, z_lo: 8; z = z_hi * 8 + z_lo), core: 2. Of those that a mesh axis runs over, the one named last changes fastest.
Arguments:
- queries: bfloat16 [64, 4, 2048], P('roll', None, 'kv'), may hold values from -8 to 8
- prompt_cache: bfloat16 [4, 16384, 1024], P(None, 'roll', 'kv'), may hold values from -4 to 4
- gen_cache: bfloat16 [64, 128, 1024], P('roll', None, 'kv'), may hold values from -4 to 4
- gen_lengths: int32 [64], P('roll'), may hold values from 1 to 128, 4096 in all
- new_kv: bfloat16 [64, 4, 1024], P('roll', None, 'kv'), may hold values from -4 to 4
- w_out: bfloat16 [2048, 2880], P('kv'), may hold values from -3 to 3
- residual: bfloat16 [64, 4, 2880], P('roll', None, 'kv'), may hold values from -10 to 10
- norm_gain: float32 [2880], P('kv'), may hold values from 0.5 to 1.5
- w_gate: bfloat16 [64, 2880, 1440], P('roll', None, 'kv'), may hold values from -0.109375 to 0.109375
- w_up: bfloat16 [64, 2880, 1440], P('roll', None, 'kv'), may hold values from -0.109375 to 0.109375
- w_down: bfloat16 [64, 1440, 2880], P('roll', 'kv'), may hold values from -0.15625 to 0.15625
- expert_ids: int32 [64, 4, 4], replicated, may hold values from 0 to 63, all different within a row; in each aligned block of 256 rows (0 to 255, 256 to 511, ..., all dimensions but the last counted through in order) at most 48 rows name the same one
- route_weights: float32 [64, 4, 4], replicated, may hold values from 0.05 to 0.5
Outputs:
- layer_out: bfloat16 [64, 4, 2880], P('roll', None, 'kv')
Inputs may be any that keep to these rules, and one draw needn't show every extreme that they name: `expert_ids`: each row names 4 different experts; over all rows no expert is named more than 48 times, and one expert exactly 48 times. `gen_lengths`: the longest is exactly 128.
All inputs are finite; a program needn't handle non-finite values. No bound on the sum of `gen_lengths` on one device may be relied on, other than what follows from the above.
Results may differ from a plain program's by a relative error of at most 0.014.
Values may be sent and summed in bfloat16 or wider, within the bound.
A program may use at most 128 MiB of HBM per device.

v0:
```python
import jax
import jax.numpy as jnp
from jax import lax
from jax.sharding import PartitionSpec as P

D = 2880
HEAD = 64
TOPK = 4
MOSTE = 48


def merged(x, axis, combine):
    everything = jax.tree.map(lambda part: lax.all_gather(part, axis), x)
    initial = jax.tree.map(lambda part: part[0], everything)

    def hop(k, so_far):
        return combine(so_far, jax.tree.map(lambda part: part[k], everything))

    return lax.fori_loop(1, lax.axis_size(axis), hop, initial)


def merge_pair(left_part, right_part):
    maxima = jnp.maximum(left_part[0], right_part[0])
    left_factor = jnp.exp(left_part[0] - maxima)
    right_factor = jnp.exp(right_part[0] - maxima)
    totals = left_part[1] * left_factor + right_part[1] * right_factor
    accumulated = left_part[2] * left_factor[..., None] + right_part[2] * right_factor[..., None]
    return (maxima, totals, accumulated)


def on_device(
    queries,
    prompt_cache,
    gen_cache,
    gen_lengths,
    new_kv,
    w_out,
    residual,
    norm_gain,
    w_gate,
    w_up,
    w_down,
    expert_ids,
    route_weights,
):
    highest = lax.Precision.HIGHEST
    samp_local, step_count, query_width = queries.shape
    prompt_count, prompt_local, kv_width = prompt_cache.shape
    kv_local = kv_width // (2 * HEAD)
    per_group = query_width // (kv_local * HEAD)
    score_scale = HEAD ** (-0.5)
    roll_index = lax.axis_index("roll")
    everyone = lax.all_gather(queries, "roll", axis=0, tiled=True)
    group_size = everyone.shape[0] // prompt_count
    query_all = everyone.reshape(prompt_count, group_size, step_count, kv_local, per_group, HEAD)
    prompt_blocks = prompt_cache.reshape(prompt_count, prompt_local, kv_local, 2, HEAD)
    scores = (
        jnp.einsum(
            "pgtkrd,pnkd->pgtkrn",
            query_all,
            prompt_blocks[:, :, :, 0],
            preferred_element_type=jnp.float32,
        )
        * score_scale
    )
    maxima = jnp.max(scores, axis=-1)
    weights = jnp.exp(scores - maxima[..., None])
    totals = jnp.sum(weights, axis=-1)
    prompt_values = prompt_blocks[:, :, :, 1].astype(jnp.float32)
    accumulated = jnp.einsum("pgtkrn,pnkd->pgtkrd", weights, prompt_values, precision=highest)
    lead_shape = (prompt_count * group_size, step_count, kv_local, per_group)
    maxima = maxima.reshape(lead_shape)
    totals = totals.reshape(lead_shape)
    accumulated = accumulated.reshape(lead_shape + (HEAD,))
    maxima, totals, accumulated = merged((maxima, totals, accumulated), "roll", merge_pair)
    row_start = roll_index * samp_local
    maxima = lax.dynamic_slice_in_dim(maxima, row_start, samp_local, 0)
    totals = lax.dynamic_slice_in_dim(totals, row_start, samp_local, 0)
    accumulated = lax.dynamic_slice_in_dim(accumulated, row_start, samp_local, 0)
    own_query = queries.reshape(samp_local, step_count, kv_local, per_group, HEAD)
    gen_blocks = gen_cache.reshape(samp_local, -1, kv_local, 2, HEAD)
    gen_span = gen_blocks.shape[1]
    gen_scores = (
        jnp.einsum(
            "stkrd,snkd->stkrn",
            own_query,
            gen_blocks[:, :, :, 0],
            preferred_element_type=jnp.float32,
        )
        * score_scale
    )
    live_mask = jnp.arange(gen_span, dtype=jnp.int32)[None, :] < gen_lengths[:, None]
    gen_scores = jnp.where(live_mask[:, None, None, None, :], gen_scores, -jnp.inf)
    fresh_kv = new_kv.reshape(samp_local, step_count, kv_local, 2, HEAD)
    new_scores = (
        jnp.einsum(
            "stkrd,sukd->stkru", own_query, fresh_kv[:, :, :, 0], preferred_element_type=jnp.float32
        )
        * score_scale
    )
    causal = jnp.arange(step_count)[None, :] <= jnp.arange(step_count)[:, None]
    new_scores = jnp.where(causal[None, :, None, None, :], new_scores, -jnp.inf)
    overall = jnp.maximum(jnp.maximum(maxima, gen_scores.max(-1)), new_scores.max(-1))
    prompt_factor = jnp.exp(maxima - overall)
    gen_w = jnp.exp(gen_scores - overall[..., None])
    new_w = jnp.exp(new_scores - overall[..., None])
    denominator = totals * prompt_factor + gen_w.sum(-1) + new_w.sum(-1)
    numerator = accumulated * prompt_factor[..., None]
    numerator = numerator + jnp.einsum(
        "stkrn,snkd->stkrd", gen_w, gen_blocks[:, :, :, 1].astype(jnp.float32), precision=highest
    )
    numerator = numerator + jnp.einsum(
        "stkru,sukd->stkrd", new_w, fresh_kv[:, :, :, 1].astype(jnp.float32), precision=highest
    )
    local_rows = samp_local * step_count
    attended = (
        (numerator / denominator[..., None]).astype(jnp.bfloat16).reshape(local_rows, query_width)
    )
    projected = jnp.dot(attended, w_out, preferred_element_type=jnp.float32)
    projected = lax.psum_scatter(
        projected.astype(jnp.bfloat16), "kv", scatter_dimension=1, tiled=True
    ).astype(jnp.float32)
    residual_sum = residual.reshape(local_rows, -1).astype(jnp.float32) + projected
    squares = lax.psum(jnp.sum(residual_sum * residual_sum, axis=1), "kv")
    inverse = lax.rsqrt(squares / D + 1e-05)
    normed = (residual_sum * inverse[:, None] * norm_gain).astype(jnp.bfloat16)
    row_total = expert_ids.shape[0] * expert_ids.shape[1]
    route_ids = expert_ids.reshape(row_total, TOPK)
    route_w = route_weights.reshape(row_total, TOPK)
    matches = route_ids == roll_index
    present = jnp.any(matches, axis=1)
    row_weight = jnp.sum(jnp.where(matches, route_w, 0.0), axis=1)
    slot_of = jnp.cumsum(present.astype(jnp.int32)) - 1
    chooser = present[None, :] & (slot_of[None, :] == jnp.arange(MOSTE, dtype=jnp.int32)[:, None])
    select_half = chooser.astype(jnp.bfloat16)
    select_full = chooser.astype(jnp.float32)
    slot_weight = jnp.dot(select_full, row_weight, precision=highest)
    whole_rows = lax.all_gather(normed, "kv", axis=1, tiled=True)
    columns = select_half
    compact = jnp.dot(
        columns,
        lax.all_gather(whole_rows, "roll", axis=0, tiled=True),
        preferred_element_type=jnp.float32,
    ).astype(jnp.bfloat16)
    gate_pre = jnp.dot(compact, w_gate[0], preferred_element_type=jnp.float32)
    up_pre = jnp.dot(compact, w_up[0], preferred_element_type=jnp.float32)
    activation = (gate_pre * jax.nn.sigmoid(1.702 * gate_pre) * (up_pre + 1.0)).astype(jnp.bfloat16)
    expert_out = (
        jnp.dot(activation, w_down[0], preferred_element_type=jnp.float32) * slot_weight[:, None]
    )
    slot_sums = lax.psum_scatter(
        expert_out.astype(jnp.bfloat16), "kv", scatter_dimension=1, tiled=True
    ).astype(jnp.float32)
    columns = select_full
    expert_mix = lax.psum_scatter(
        lax.dot_general(columns, slot_sums, (((0,), (0,)), ((), ())), precision=highest),
        "roll",
        scatter_dimension=0,
        tiled=True,
    )
    return (residual_sum + expert_mix).astype(jnp.bfloat16).reshape(samp_local, step_count, -1)


def solution(mesh):
    in_specs = (
        P("roll", None, "kv"),
        P(None, "roll", "kv"),
        P("roll", None, "kv"),
        P("roll"),
        P("roll", None, "kv"),
        P("kv", None),
        P("roll", None, "kv"),
        P("kv"),
        P("roll", None, "kv"),
        P("roll", None, "kv"),
        P("roll", "kv", None),
        P(),
        P(),
    )
    out_specs = P("roll", None, "kv")
    return jax.shard_map(
        on_device, mesh=mesh, in_specs=in_specs, out_specs=out_specs, check_vma=False
    )
```

profile of v0, /device:TPU:1, one launch (start us, length us, event | category | flops | bytes accessed | tf_op | source)
XLA Modules:
  0.0 2214.8 jit_solution(90229492891172199)
XLA Ops:
  6.5 166.3 %all_gather.18 = bf16[64,4,256]{2,1,0:T(4,128)(2,1)S(1)} all-gather(bf16[1,4,256]{2,1,0:T(4,128)(2,1)} %param.15), channel_id=1, replica_groups=mesh['roll'=64,'kv'=8] {'roll'}, dimensions={0}, use_global_device_ids=true | all-gather | bytes 133120 | tf_op jit(solution)/shard_map/all_gather | solution.py:53
  177.8 1.3 dynamic-slice
  180.0 170.3 %all_gather.19 = f32[64,64,4,1,4]{1,4,3,2,0:T(4,128)S(1)} all-gather(f32[1,64,4,1,4]{1,4,3,2,0:T(4,128)S(1)} %all_gather_reshape.9), channel_id=1, replica_groups=mesh['roll'=64,'kv'=8] {'roll'}, dimensions={0}, use_global_device_ids=true | all-gather | bytes 266240 | tf_op jit(solution)/shard_map/all_gather | solution.py:13
  350.2 250.1 %all_gather.20 = f32[64,64,4,1,4]{1,4,3,2,0:T(4,128)} all-gather(f32[1,64,4,1,4]{1,4,3,2,0:T(4,128)S(1)} %bitcast.228), channel_id=1, replica_groups=mesh['roll'=64,'kv'=8] {'roll'}, dimensions={0}, use_global_device_ids=true | all-gather | bytes 266240 | tf_op jit(solution)/shard_map/all_gather | solution.py:13
  602.6 210.1 %while.19 = (s32[]{:T(128)}, f32[64,4,1,4]{0,3,2,1:T(4,128)S(1)}, f32[64,4,1,4]{0,3,2,1:T(4,128)S(1)}, f32[64,4,1,4,64]{4,3,2,1,0:T(4,128)S(1)}, f32[64,64,4,1,4...) while((s32[]{:T(128)}, f32[64,4,1,4]{0,3,2,1:T(4,128)S(1)}, ...), condition=%wide.region_3.0_spmd, body=%wide.region_2.0_spmd.sunk | while | flops 203781 | bytes 1388699 | solution.py:19
  614.8 1.2 fusion.76
  634.8 1.2 fusion.76
  658.1 1.2 fusion.76
  678.1 1.2 fusion.76
  698.2 1.2 fusion.76
  721.5 1.2 fusion.76
  741.5 1.2 fusion.76
  761.5 1.2 fusion.76
  814.5 43.4 %all-reduce = bf16[4,2880]{1,0:T(4,128)(2,1)S(1)} all-reduce(bf16[4,2880]{1,0:T(4,128)(2,1)S(1)} %convolution_convert_fusion.1), channel_id=2, replica_groups=mesh['roll'=64,'kv'=8] {'kv'}, use_global_device_ids=true, to_apply=%region_8.9.clone | all-reduce | flops 11520 | bytes 46080
  858.1 21.5 psum.7
  879.7 39.6 %all-gather = bf16[8,360,4]{1,2,0:T(4,128)(2,1)S(1)} all-gather(bf16[1,360,4]{1,2,0:T(4,128)(2,1)S(1)} %fusion.52), channel_id=1, replica_groups=mesh['roll'=64,'kv'=8] {'kv'}, dimensions={0}, use_global_device_ids=true | all-gather | bytes 25920 | tf_op jit(solution)/shard_map/all_gather | solution.py:138
  921.6 119.1 %all-gather.7.cloned.1.call-done = bf16[64,4,2880]{2,1,0:T(4,128)(2,1)} async-done(((bf16[1,4,2880]{2,1,0:T(4,128)(2,1)}), bf16[64,4,2880]{2,1,0:T(4,128)(2,1)}) %all-gather.7.cloned.1.call-update) | async-done | bytes 1474576 | tf_op jit(solution)/shard_map/all_gather | solution.py:142
  1040.7 2.6 reshape.214
  1045.8 2.9 fusion.6
  1048.8 103.2 %all-reduce.6.cloned.1.call-done = bf16[48,2880]{1,0:T(8,128)(2,1)} async-done(((bf16[48,2880]{1,0:T(8,128)(2,1)}), bf16[48,2880]{1,0:T(8,128)(2,1)}) %all-reduce.6.cloned.1.call-update) | async-done | bytes 276496
  1152.0 1.8 fusion.33
  1153.9 1.3 dynamic-slice.4
  1155.8 1051.1 %all-reduce.8.cloned.1.call-done = f32[256,360]{1,0:T(8,128)} async-done(((f32[256,360]{1,0:T(8,128)}), f32[256,360]{1,0:T(8,128)}) %all-reduce.8.cloned.1.call-update) | async-done | bytes 368656
  2206.9 1.4 fusion.53
  (518 shorter events, 210.0 us)
Async XLA Ops:
  6.5 807.4 %copy-start = (bf16[256,2880]{0,1:T(8,128)(2,1)S(1)}, bf16[256,2880]{0,1:T(8,128)(2,1)}, u32[]{:S(2)}) copy-start(bf16[256,2880]{0,1:T(8,128)(2,1)} %param.20) | copy-start | bytes 4423684
  6.5 594.7 %all-gather.5.cloned.1.call-start = ((), (), s32[]{:S(2)}) async-start(), calls=%async_computation | async-start | bytes 34078720 | tf_op jit(solution)/shard_map/all_gather | solution.py:13
  175.2 1.0 copy-start.5
  176.1 0.8 copy-start.9
  176.1 0.9 copy-start.3
  176.1 864.6 %all-gather.7.cloned.1.call-start = ((), (), s32[]{:S(2)}) async-start(), calls=%async_computation.1 | async-start | bytes 1530880 | tf_op jit(solution)/shard_map/all_gather | solution.py:142
  812.8 45.1 %copy-start.4 = (bf16[1,4,360]{2,1,0:T(4,128)(2,1)S(1)}, bf16[1,4,360]{2,1,0:T(4,128)(2,1)}, u32[]{:S(2)}) copy-start(bf16[1,4,360]{2,1,0:T(4,128)(2,1)} %param.21) | copy-start | bytes 8644
  812.8 66.9 %copy-start.8 = (f32[360]{0:T(512)S(1)}, f32[360]{0:T(512)}, u32[]{:S(2)}) copy-start(f32[360]{0:T(512)} %param.22) | copy-start | bytes 4324
  812.9 107.2 %copy-start.6 = (f32[64,4,4]{0,2,1:T(4,128)S(1)}, f32[64,4,4]{0,2,1:T(4,128)}, u32[]{:S(2)}) copy-start(f32[64,4,4]{0,2,1:T(4,128)} %param.27) | copy-start | bytes 12292
  812.9 107.2 %copy-start.7 = (s32[64,4,4]{0,2,1:T(4,128)S(1)}, s32[64,4,4]{0,2,1:T(4,128)}, u32[]{:S(2)}) copy-start(s32[64,4,4]{0,2,1:T(4,128)} %param.26) | copy-start | bytes 12292
  920.1 231.9 %all-reduce.6.cloned.1.call-start = ((), (), s32[]{:S(2)}) async-start(), calls=%async_computation.2 | async-start | bytes 565248
  1043.4 1.2 copy-start.2
  1044.6 1.2 copy-start.1
  1048.8 1158.2 %all-reduce.8.cloned.1.call-start = ((), (), s32[]{:S(2)}) async-start(), calls=%async_computation.3 | async-start | bytes 786432
Sparse Core Ops, SparseCore 0:
  176.3 423.3 all-gather.4
  920.2 120.4 all-gather.6
  1048.9 103.0 all-reduce.5
  1155.0 1051.8 all-reduce.7
where the time goes:
time: 2220 us; the launch traced here: 2210 us
  waiting for transfers between devices  1270 us (57%)
  blocking collectives  691 us (31%)
  other arithmetic  124 us (6%)
  local copies, waits for them, and re-layouts  98.2 us (4%)
    unnamed x6, waiting for transfers between devices  1150 us
    all_gather x2, blocking collectives, merged(): everything = jax.tree.map(lambda part: lax.all_gather(part, axis), x)  420 us
    all_gather x1, blocking collectives, on_device(): everyone = lax.all_gather(queries, 'roll', axis=0, tiled=True)  166 us
    all_gather x1, waiting for transfers between devices, on_device(): lax.all_gather(whole_rows, 'roll', axis=0, tiled=True)  119 us
    add x63, other arithmetic, merge_pair(): left_part[2] * left_factor[..., None]  74.7 us
    dynamic_slice x63, local copies, waits for them, and re-layouts, hop(): return combine(so_far, jax.tree.map(lambda part: part[k], everything))  68.2 us
    mul x63, other arithmetic, merge_pair(): right_part[2] * right_factor[..., None]  45.8 us
  transfers between devices with their start and end apart: 4, of which 3 were waited for; matrix products, arithmetic and copies ran while one was open for 0% of the time, Pallas kernels for 0%

commit v1 on v0

v1 whole, which is shorter than its diff:
```python
import jax
import jax.numpy as jnp
from jax import lax
from jax.experimental import pallas as pl
from jax.experimental.pallas import tpu as pltpu
from jax.sharding import PartitionSpec as P

D = 2880
HEAD = 64
MOSTE = 48
KV = 8
NX, NZ, NY, NC = 4, 2, 4, 2
SLICE = D // KV
LANES = 384
QUARTER = 720
WIDE = 768
PADDED = 2944
F32 = jnp.float32
BF16 = jnp.bfloat16
MESH = pl.DeviceIdType.MESH


def iota(shape, axis):
    return lax.broadcasted_iota(jnp.int32, shape, axis)


def onehot(mask):
    return jnp.where(mask, 1.0, 0.0).astype(BF16)


def dot(a, b, dims=((1,), (0,))):
    return lax.dot_general(a, b, (dims, ((), ())), preferred_element_type=F32)


def packed(m, l, acc):
    lane = iota(acc.shape, 1)
    return jnp.where(lane == 0, m, jnp.where(lane == 1, l, jnp.where(lane >= HEAD, acc, 0.0)))


def merge(rows):
    top = rows[0][:, 0:1]
    for r in rows[1:]:
        top = jnp.maximum(top, r[:, 0:1])
    total = rows[0] * jnp.exp(rows[0][:, 0:1] - top)
    for r in rows[1:]:
        total = total + r * jnp.exp(r[:, 0:1] - top)
    return jnp.where(iota(total.shape, 1) == 0, top, total)


def window(ref, k):
    start = SLICE * k // 128 * 128
    wide = ref[:, start:start + 512]
    shift = SLICE * k - start
    if shift:
        wide = pltpu.roll(wide, 512 - shift, 1)
    return wide[:, :LANES]


def kernel(
    q_ref, prompt_ref, gen_ref, new_ref, len_ref, wout_ref, res_ref, gain_ref,
    wg_ref, wu_ref, wd_ref, ids_ref, rw_ref, out_ref,
    qbuf, part, rc, s1, rx, s2, ry, s3, rz,
    proj, rsend, rrecv, agbuf, blk, ybuf, choose, shift_ref,
    oflat, esend, erecv, dn, r1, e1, rx2, e2, ry2, e3, rz2,
    send_sem, recv_sem,
):
    roll = lax.axis_index("roll")
    kv = lax.axis_index("kv")
    c = lax.rem(roll, NC)
    y = lax.rem(roll // NC, NY)
    z = lax.rem(roll // (NC * NY), NZ)
    x = roll // (NC * NY * NZ)

    def at(xx, zz, yy, cc):
        return (((xx * NZ + zz) * NY + yy) * NC + cc, kv)

    to_core = at(x, z, y, 1 - c)
    to_z = at(x, 1 - z, y, c)
    to_x = [at(lax.rem(x + d, NX), z, y, c) for d in range(1, NX)]
    to_y = [at(x, z, lax.rem(y + d, NY), c) for d in range(1, NY)]
    to_kv = [(roll, lax.rem(kv + d, KV)) for d in range(1, KV)]
    partners = [to_core, to_z] + to_x + to_y + to_kv
    barrier = pltpu.get_barrier_semaphore()
    for device in partners:
        pl.semaphore_signal(barrier, inc=1, device_id=device, device_id_type=MESH)

    next_sem = [0]

    def start(src, dst, device):
        i = next_sem[0]
        next_sem[0] += 1
        copy = pltpu.make_async_remote_copy(
            src_ref=src, dst_ref=dst, send_sem=send_sem.at[i], recv_sem=recv_sem.at[i],
            device_id=device, device_id_type=MESH,
        )
        copy.start()
        return copy

    def finish(copies):
        for copy in copies:
            copy.wait()

    def gather(buf):
        finish([start(buf.at[c, x, y, z], buf.at[c, x, y, z], to_z)])
        finish([start(buf.at[c, x, y], buf.at[c, x, y], device) for device in to_y])
        finish([start(buf.at[c, x], buf.at[c, x], device) for device in to_x])
        finish([start(buf.at[c], buf.at[c], to_core)])

    qbuf[c, x, y, z] = q_ref[...]

    match = ids_ref[...] == roll
    present = jnp.max(jnp.where(match, 1.0, 0.0), axis=0, keepdims=True)
    row_weight = jnp.sum(jnp.where(match, rw_ref[...], 0.0), axis=0, keepdims=True)
    present = jnp.broadcast_to(present, (16, 256))
    upto = onehot(iota((256, 256), 0) <= iota((256, 256), 1))
    slot = jnp.where(present > 0.5, dot(present.astype(BF16), upto) - 1.0, -1.0)
    row, col = iota((256, 1024), 0), iota((256, 1024), 1)
    spread = onehot(((row >> 2) == (col >> 4)) & ((row & 3) == (col & 3)))
    slot_wide = dot(slot.astype(BF16), spread)[0:1]
    lane = iota((1, 1024), 1)
    code = slot_wide + MOSTE * ((lane >> 2) & 3).astype(F32)
    code = jnp.where(slot_wide < -0.5, -1.0, code)
    choose[...] = onehot(iota((4 * MOSTE, 1024), 0) == code.astype(jnp.int32))
    chosen = iota((MOSTE, 256), 0) == slot[0:1].astype(jnp.int32)
    slot_weight = jnp.sum(jnp.where(chosen, row_weight, 0.0), axis=1, keepdims=True)
    back = onehot(chosen)
    row, col = iota((WIDE, WIDE), 0), iota((WIDE, WIDE), 1)
    shift_ref[...] = onehot(
        ((row < SLICE) & (col == row))
        | ((row >= LANES) & (row < LANES + SLICE) & (col == row - (LANES - SLICE)))
    )

    own = q_ref[...]
    live = iota((16, 128), 1) < len_ref[0]
    gen_s = jnp.where(live, dot(own, gen_ref[...], ((1,), (1,))), -1e30)
    causal = iota((16, 16), 1) <= (iota((16, 16), 0) & 3)
    new_s = jnp.where(causal, dot(own, new_ref[...], ((1,), (1,))), -1e30)
    top = jnp.maximum(
        jnp.max(gen_s, axis=1, keepdims=True), jnp.max(new_s, axis=1, keepdims=True)
    )
    gen_w = jnp.exp(gen_s - top)
    new_w = jnp.exp(new_s - top)
    own_part = packed(
        top,
        jnp.sum(gen_w, axis=1, keepdims=True) + jnp.sum(new_w, axis=1, keepdims=True),
        dot(gen_w.astype(BF16), gen_ref[...]) + dot(new_w.astype(BF16), new_ref[...]),
    )
    pl.semaphore_wait(barrier, len(partners))

    gather(qbuf)
    for cc in range(NC):
        for xx in range(NX):
            q = qbuf[cc, xx].reshape(128, 128)
            keys = prompt_ref[xx]
            s = dot(q, keys, ((1,), (1,)))
            m = jnp.max(s, axis=1, keepdims=True)
            w = jnp.exp(s - m)
            l = jnp.sum(w, axis=1, keepdims=True)
            part[cc, xx] = packed(m, l, dot(w.astype(BF16), keys)).reshape(NY, NZ, 16, 128)
    part[c, x, y, z] = merge([part[c, x, y, z], own_part])

    finish([start(part.at[1 - c], rc, to_core)])
    s1[...] = merge([part[c].reshape(512, 128), rc[...].reshape(512, 128)]).reshape(s1.shape)
    finish([
        start(s1.at[lax.rem(x + d, NX)], rx.at[d - 1], to_x[d - 1]) for d in range(1, NX)
    ])
    s2[...] = merge(
        [s1[x].reshape(128, 128)] + [rx[d].reshape(128, 128) for d in range(NX - 1)]
    ).reshape(s2.shape)
    finish([
        start(s2.at[lax.rem(y + d, NY)], ry.at[d - 1], to_y[d - 1]) for d in range(1, NY)
    ])
    s3[...] = merge(
        [s2[y].reshape(32, 128)] + [ry[d].reshape(32, 128) for d in range(NY - 1)]
    ).reshape(s3.shape)
    finish([start(s3.at[1 - z], rz, to_z)])
    final = merge([s3[z], rz[...]])
    lane = iota((16, 128), 1)
    attended = jnp.where(lane >= HEAD, final / final[:, 1:2], 0.0).astype(BF16)

    row, col = iota((128, 256), 0), iota((128, 256), 1)
    copies = onehot((row >= HEAD) & ((col & (HEAD - 1)) == row - HEAD))
    heads = dot(attended, copies)
    heads = jnp.where((iota((16, 256), 0) >> 2) == (iota((16, 256), 1) >> 6), heads, 0.0)
    steps = onehot((iota((16, 16), 1) & 3) == iota((16, 16), 0))
    attended = dot(steps, heads.astype(BF16)).astype(BF16)
    proj[:, PADDED - 128:] = jnp.zeros((8, 128), F32)
    proj[:, :D] = dot(attended, wout_ref[...])[0:8]
    for k in range(KV):
        rsend[k] = window(proj, k).astype(BF16)
    finish([
        start(rsend.at[lax.rem(kv + d, KV)], rrecv.at[d - 1], to_kv[d - 1])
        for d in range(1, KV)
    ])
    projected = rsend[kv].astype(F32)
    for d in range(KV - 1):
        projected = projected + rrecv[d].astype(F32)
    lane = iota((8, LANES), 1)
    residual_sum = jnp.where(lane < SLICE, res_ref[...] + projected, 0.0)

    squares = jnp.sum(residual_sum * residual_sum, axis=1, keepdims=True)
    high = squares.astype(BF16).astype(F32)
    scaled = residual_sum * gain_ref[...]
    agbuf[kv] = jnp.where(
        lane == SLICE, high, jnp.where(lane == SLICE + 1, squares - high, scaled)
    ).astype(BF16)
    finish([start(agbuf.at[kv], agbuf.at[kv], device) for device in to_kv])
    squares = jnp.zeros((8, 1), F32)
    for k in range(KV):
        piece = agbuf[k].astype(F32)
        squares = squares + piece[:, SLICE:SLICE + 1] + piece[:, SLICE + 1:SLICE + 2]
        half = LANES * (k % 2)
        blk[4 * (k // 2):4 * (k // 2) + 4, half:half + LANES] = piece[0:4]
    inverse = lax.rsqrt(squares / D + 1e-05)
    inverse = jnp.concatenate([inverse, inverse], axis=0)
    high = inverse.astype(BF16).astype(F32)
    block = dot(blk[...].astype(BF16), shift_ref[...])
    lane = iota((16, WIDE), 1)
    ybuf[c, x, y, z] = jnp.where(
        lane == QUARTER, high, jnp.where(lane == QUARTER + 1, inverse - high, block)
    ).astype(BF16)
    gather(ybuf)

    rows = dot(choose[...], ybuf[...].reshape(1024, WIDE))
    factor = rows[0:MOSTE, QUARTER:QUARTER + 1] + rows[0:MOSTE, QUARTER + 1:QUARTER + 2]
    gate = jnp.zeros((MOSTE, wg_ref.shape[1]), F32)
    up = jnp.zeros((MOSTE, wg_ref.shape[1]), F32)
    for j in range(4):
        features = rows[MOSTE * j:MOSTE * (j + 1), :QUARTER].astype(BF16)
        gate = gate + dot(features, wg_ref[QUARTER * j:QUARTER * (j + 1), :])
        up = up + dot(features, wu_ref[QUARTER * j:QUARTER * (j + 1), :])
    gate = gate * factor
    up = up * factor
    activation = (gate * jax.nn.sigmoid(1.702 * gate) * (up + 1.0)).astype(BF16)
    oflat[:, PADDED - 128:] = jnp.zeros((MOSTE, 128), F32)
    oflat[:, :D] = dot(activation, wd_ref[...]) * slot_weight
    for k in range(KV):
        esend[k] = window(oflat, k).astype(BF16)
    finish([
        start(esend.at[lax.rem(kv + d, KV)], erecv.at[d - 1], to_kv[d - 1])
        for d in range(1, KV)
    ])
    summed = esend[kv].astype(F32)
    for d in range(KV - 1):
        summed = summed + erecv[d].astype(F32)

    dense = dot(back, summed.astype(BF16), ((0,), (0,)))
    dn[...] = dense.astype(BF16).reshape(dn.shape)
    finish([start(dn.at[1 - c], r1, to_core)])
    e1[...] = (dn[c].astype(F32) + r1[...].astype(F32)).reshape(e1.shape)
    finish([
        start(e1.at[lax.rem(x + d, NX)], rx2.at[d - 1], to_x[d - 1]) for d in range(1, NX)
    ])
    e2[...] = (e1[x] + rx2[0] + rx2[1] + rx2[2]).reshape(e2.shape)
    finish([
        start(e2.at[lax.rem(y + d, NY)], ry2.at[d - 1], to_y[d - 1]) for d in range(1, NY)
    ])
    e3[...] = e2[y] + ry2[0] + ry2[1] + ry2[2]
    finish([start(e3, rz2, to_z)])
    mix = e3[...] + rz2[...]
    mix = jnp.where(z == 0, mix, pltpu.roll(mix, 4, 0))
    out_ref[...] = residual_sum + mix


def on_device(
    queries, prompt_cache, gen_cache, gen_lengths, new_kv, w_out, residual, norm_gain,
    w_gate, w_up, w_down, expert_ids, route_weights,
):
    steps = queries.shape[1]
    q = queries.reshape(steps, 4, HEAD).transpose(1, 0, 2).reshape(4 * steps, HEAD)
    q = jnp.pad(q * BF16(0.125), ((0, 0), (0, HEAD)))
    fresh = jnp.pad(new_kv[0], ((0, 16 - steps), (0, 0)))
    res = jnp.pad(residual[0].astype(F32), ((0, 8 - steps), (0, LANES - SLICE)))
    gain = jnp.pad(norm_gain, (0, LANES - SLICE)).reshape(1, LANES)

    def by_device(a):
        a = a.reshape(NX, NZ, NY, NC, steps, 4)
        return a.transpose(5, 3, 0, 2, 1, 4).reshape(4, -1)

    vmem = pl.BlockSpec(memory_space=pltpu.VMEM)
    smem = pl.BlockSpec(memory_space=pltpu.SMEM)
    grid = (NC, NX, NY, NZ)
    ffe = w_gate.shape[2]
    scratch = [
        pltpu.VMEM(grid + (16, 128), BF16),
        pltpu.VMEM(grid + (16, 128), F32),
        pltpu.VMEM((NX, NY, NZ, 16, 128), F32),
        pltpu.VMEM((NX, NY, NZ, 16, 128), F32),
        pltpu.VMEM((NX - 1, NY, NZ, 16, 128), F32),
        pltpu.VMEM((NY, NZ, 16, 128), F32),
        pltpu.VMEM((NY - 1, NZ, 16, 128), F32),
        pltpu.VMEM((NZ, 16, 128), F32),
        pltpu.VMEM((16, 128), F32),
        pltpu.VMEM((8, PADDED), F32),
        pltpu.VMEM((KV, 8, LANES), BF16),
        pltpu.VMEM((KV - 1, 8, LANES), BF16),
        pltpu.VMEM((KV, 8, LANES), BF16),
        pltpu.VMEM((16, WIDE), F32),
        pltpu.VMEM(grid + (16, WIDE), BF16),
        pltpu.VMEM((4 * MOSTE, 1024), BF16),
        pltpu.VMEM((WIDE, WIDE), BF16),
        pltpu.VMEM((MOSTE, PADDED), F32),
        pltpu.VMEM((KV, MOSTE, LANES), BF16),
        pltpu.VMEM((KV - 1, MOSTE, LANES), BF16),
        pltpu.VMEM((NC, 128, LANES), BF16),
        pltpu.VMEM((128, LANES), BF16),
        pltpu.VMEM((NX, 32, LANES), F32),
        pltpu.VMEM((NX - 1, 32, LANES), F32),
        pltpu.VMEM((NY, 8, LANES), F32),
        pltpu.VMEM((NY - 1, 8, LANES), F32),
        pltpu.VMEM((8, LANES), F32),
        pltpu.VMEM((8, LANES), F32),
        pltpu.SemaphoreType.DMA((64,)),
        pltpu.SemaphoreType.DMA((64,)),
    ]
    out = pl.pallas_call(
        kernel,
        out_shape=jax.ShapeDtypeStruct((8, LANES), F32),
        in_specs=[vmem] * 4 + [smem] + [vmem] * 8,
        out_specs=vmem,
        scratch_shapes=scratch,
        compiler_params=pltpu.CompilerParams(
            collective_id=0, has_side_effects=True, vmem_limit_bytes=56 * 1024 * 1024
        ),
        name="layer",
    )(
        q, prompt_cache, gen_cache[0], fresh, gen_lengths, w_out, res, gain,
        w_gate.reshape(D, ffe), w_up.reshape(D, ffe), w_down.reshape(ffe, D),
        by_device(expert_ids), by_device(route_weights),
    )
    return out[:steps, :SLICE].astype(BF16)[None]


def solution(mesh):
    in_specs = (
        P("roll", None, "kv"),
        P(None, "roll", "kv"),
        P("roll", None, "kv"),
        P("roll"),
        P("roll", None, "kv"),
        P("kv", None),
        P("roll", None, "kv"),
        P("kv"),
        P("roll", None, "kv"),
        P("roll", None, "kv"),
        P("roll", "kv", None),
        P(),
        P(),
    )
    out_specs = P("roll", None, "kv")
    return jax.shard_map(
        on_device, mesh=mesh, in_specs=in_specs, out_specs=out_specs, check_vma=False
    )
```

time: 2220 us -> 137 us (0.06)
  the two profiles are of different devices: /device:TPU:1 before, /device:TPU:64 now
where the time goes in v1:
time: 137 us
  Pallas kernels  120 us (88%)
  local copies, waits for them, and re-layouts  14 us (10%)
  other arithmetic  1.97 us (1%)
    pallas_call x1, Pallas kernels, on_device(): pl.pallas_call(kernel, out_shape=jax.ShapeDtypeStruct((8, LANES), F32), i...  120 us
    unnamed x11, local copies, waits for them, and re-layouts  6.67 us

profile of v1, /device:TPU:64, one launch (start us, length us, event | category | flops | bytes accessed | tf_op | source)
XLA Modules:
  0.0 136.6 jit_solution(12299098215522479230)
XLA Ops:
  0.0 0.0 copy-start.1
  0.7 0.7 broadcast_multiply_fusion
  1.4 0.1 mul.17
  1.5 0.6 pad.18.q_ref
  2.1 0.7 pad.22
  2.8 0.6 reshape.32.gain_ref
  3.4 1.3 pad.19.new_ref
  4.7 1.3 pad_convert_fusion.res_ref
  5.9 0.8 copy.23
  6.8 0.6 copy.24
  7.4 0.8 reshape.37.ids_ref
  8.2 0.8 copy.25
  9.0 0.0 copy-start.2
  9.0 0.6 copy.26
  9.6 0.8 reshape.39.rw_ref
  10.4 0.0 copy-done.1
  10.4 1.7 %copy.21 = bf16[1,2880,180]{2,1,0:T(8,128)(2,1)} copy(bf16[1,2880,180]{1,2,0:T(8,128)(2,1)S(1)} %copy-done.1) | data formatting | bytes 2073600 | tf_op args[8]
  12.1 0.0 copy-start
  12.1 0.0 copy-done.2
  12.1 1.7 %copy.22 = bf16[1,2880,180]{2,1,0:T(8,128)(2,1)} copy(bf16[1,2880,180]{1,2,0:T(8,128)(2,1)S(1)} %copy-done.2) | data formatting | bytes 2073600 | tf_op args[9]
  13.7 0.0 copy-done
  13.7 1.7 %copy.27.wout_ref = bf16[256,2880]{1,0:T(8,128)(2,1)} copy(bf16[256,2880]{0,1:T(8,128)(2,1)S(1)} %copy-done) | data formatting | bytes 2949120 | tf_op args[5]
  15.5 119.9 %layer.1 = f32[8,384]{1,0:T(8,128)} custom-call(bf16[16,128]{1,0:T(8,128)(2,1)} %pad.18.q_ref, bf16[4,256,128]{2,1,0:T(8,128)(2,1)} %prompt_ref.1, bf16[128,128]{1,0:T(8,128)(2,1)} %bitcast.22, bf16[16,128]{1,0:T(8,128)(2,1)} %pad.19.new_ref, s32[1]{0:T(128)S(6)} %copy.28.len_ref, bf16[256,2880]{1,0:T(8,128)(2,1)} %copy.27.wout_ref, ...), custom_call_target="tpu_custom_call" | custom-call | tf_op jit(solution)/shard_map/layer/pallas_call | solution.py:316
  135.4 1.3 fusion
  (1 shorter events, 0.0 us)
Async XLA Ops:
  0.0 10.4 %copy-start.1 = (bf16[1,2880,180]{1,2,0:T(8,128)(2,1)S(1)}, bf16[1,2880,180]{1,2,0:T(8,128)(2,1)}, u32[]{:S(2)}) copy-start(bf16[1,2880,180]{1,2,0:T(8,128)(2,1)} %param.21) | copy-start | bytes 3110404
  9.0 3.1 %copy-start.2 = (bf16[1,2880,180]{1,2,0:T(8,128)(2,1)S(1)}, bf16[1,2880,180]{1,2,0:T(8,128)(2,1)}, u32[]{:S(2)}) copy-start(bf16[1,2880,180]{1,2,0:T(8,128)(2,1)} %param.22) | copy-start | bytes 3110404
  12.1 1.7 %copy-start = (bf16[256,2880]{0,1:T(8,128)(2,1)S(1)}, bf16[256,2880]{0,1:T(8,128)(2,1)}, u32[]{:S(2)}) copy-start(bf16[256,2880]{0,1:T(8,128)(2,1)} %param.18) | copy-start | bytes 4423684

commit v2 on v1

v2 whole, which is shorter than its diff:
```python
import jax
import jax.numpy as jnp
from jax import lax
from jax.experimental import pallas as pl
from jax.experimental.pallas import tpu as pltpu
from jax.sharding import PartitionSpec as P

D = 2880
HEAD = 64
MOSTE = 48
KV = 8
NX, NZ, NY, NC = 4, 2, 4, 2
SLICE = D // KV
LANES = 384
QUARTER = 720
WIDE = 768
PADDED = 2944
F32 = jnp.float32
BF16 = jnp.bfloat16
MESH = pl.DeviceIdType.MESH


def iota(shape, axis):
    return lax.broadcasted_iota(jnp.int32, shape, axis)


def onehot(mask):
    return jnp.where(mask, 1.0, 0.0).astype(BF16)


def dot(a, b, dims=((1,), (0,))):
    return lax.dot_general(a, b, (dims, ((), ())), preferred_element_type=F32)


def packed(m, l, acc):
    lane = iota(acc.shape, 1)
    return jnp.where(lane == 0, m, jnp.where(lane == 1, l, jnp.where(lane >= HEAD, acc, 0.0)))


def merge(rows):
    top = rows[0][:, 0:1]
    for r in rows[1:]:
        top = jnp.maximum(top, r[:, 0:1])
    total = rows[0] * jnp.exp(rows[0][:, 0:1] - top)
    for r in rows[1:]:
        total = total + r * jnp.exp(r[:, 0:1] - top)
    return jnp.where(iota(total.shape, 1) == 0, top, total)


def window(ref, k):
    start = SLICE * k // 128 * 128
    wide = ref[:, start:start + 512]
    shift = SLICE * k - start
    if shift:
        wide = pltpu.roll(wide, 512 - shift, 1)
    return wide[:, :LANES]


def kernel(
    q_ref, prompt_hbm, gen_hbm, new_ref, len_ref, wout_hbm, res_ref, gain_ref,
    wg_hbm, wu_hbm, wd_hbm, ids_ref, rw_ref, out_ref,
    prompt_ref, gen_ref, wout_ref, wg_ref, wu_ref, wd_ref,
    padq, padn, padr, padg, pres,
    qbuf, part, rc, s1, rx, s2, ry, s3, rz,
    proj, rsend, rrecv, agbuf, blk, ybuf, choose, shift_ref, xs,
    oflat, esend, erecv, dn, r1, e1, rx2, e2, ry2, e3, rz2,
    send_sem, recv_sem, load_sem,
):
    roll = lax.axis_index("roll")
    kv = lax.axis_index("kv")
    c = lax.rem(roll, NC)
    y = lax.rem(roll // NC, NY)
    z = lax.rem(roll // (NC * NY), NZ)
    x = roll // (NC * NY * NZ)

    def at(xx, zz, yy, cc):
        return (((xx * NZ + zz) * NY + yy) * NC + cc, kv)

    to_core = at(x, z, y, 1 - c)
    to_z = at(x, 1 - z, y, c)
    to_x = [at(lax.rem(x + d, NX), z, y, c) for d in range(1, NX)]
    to_y = [at(x, z, lax.rem(y + d, NY), c) for d in range(1, NY)]
    to_kv = [(roll, lax.rem(kv + d, KV)) for d in range(1, KV)]
    column = z * KV + kv
    to_column = []
    for d in range(1, NZ * KV):
        there = lax.rem(column + d, NZ * KV)
        to_column.append((at(x, there // KV, y, c)[0], lax.rem(there, KV)))
    partners = [to_core] + to_x + to_y + to_column
    barrier = pltpu.get_barrier_semaphore()
    for device in partners:
        pl.semaphore_signal(barrier, inc=1, device_id=device, device_id_type=MESH)

    loads = [
        pltpu.make_async_copy(src, dst, load_sem.at[i])
        for i, (src, dst) in enumerate([
            (gen_hbm, gen_ref), (prompt_hbm, prompt_ref), (wout_hbm, wout_ref),
            (wg_hbm, wg_ref), (wu_hbm, wu_ref), (wd_hbm, wd_ref),
        ])
    ]
    for load in loads:
        load.start()

    next_sem = [0]

    def start(src, dst, device):
        i = next_sem[0]
        next_sem[0] += 1
        copy = pltpu.make_async_remote_copy(
            src_ref=src, dst_ref=dst, send_sem=send_sem.at[i], recv_sem=recv_sem.at[i],
            device_id=device, device_id_type=MESH,
        )
        copy.start()
        return copy

    def finish(copies):
        for copy in copies:
            copy.wait()

    padq[...] = jnp.zeros((16, 256), F32)
    padq[0:4, :] = q_ref[...].astype(F32) * 0.125
    row, col = iota((128, 256), 0), iota((128, 256), 1)
    own_head = (iota((16, 256), 0) >> 2) == (iota((16, 256), 1) >> 6)
    each = dot(onehot((iota((16, 16), 0) & 3) == iota((16, 16), 1)), padq[...].astype(BF16))
    each = jnp.where(own_head, each, 0.0).astype(BF16)
    fold = onehot((row < HEAD) & ((col & (HEAD - 1)) == row))
    own = dot(each, fold, ((1,), (1,))).astype(BF16)
    qbuf[z, c, x, y] = own

    pres[...] = jnp.zeros((16, 64), F32)
    weights = []
    for t in range(4):
        match = ids_ref[t] == roll
        pres[t:t + 1, :] = jnp.max(jnp.where(match, 1.0, 0.0), axis=0, keepdims=True)
        weights.append(jnp.sum(jnp.where(match, rw_ref[t], 0.0), axis=0, keepdims=True))
    present = pres[...]
    upto = onehot(iota((64, 64), 0) <= iota((64, 64), 1))
    earlier = onehot(iota((16, 16), 1) < iota((16, 16), 0))
    totals = jnp.broadcast_to(jnp.sum(present, axis=1, keepdims=True), (16, 64))
    slot = dot(present.astype(BF16), upto) + dot(earlier, totals.astype(BF16)) - 1.0
    slot = jnp.where(present > 0.5, slot, -1.0)
    slot_half = slot.astype(BF16)

    def place(sample):
        return (
            (((sample >> 3) & 1) << 5) | ((sample & 1) << 4)
            | ((sample >> 4) << 2) | ((sample >> 1) & 3)
        )

    spread = onehot(place(iota((64, 1024), 0)) == (iota((64, 1024), 1) >> 4))
    wide = dot(slot_half, spread)
    wide = jnp.where(iota((16, 1024), 0) == (iota((16, 1024), 1) & 3), wide, 0.0)
    wide = jnp.sum(wide, axis=0, keepdims=True)
    lane = iota((1, 1024), 1)
    code = jnp.where(wide < -0.5, -1.0, wide + MOSTE * ((lane >> 2) & 3).astype(F32))
    choose[...] = onehot(iota((4 * MOSTE, 1024), 0) == code.astype(jnp.int32))
    spread = onehot(place(iota((64, 256), 0)) == (iota((64, 256), 1) >> 2))
    wide = dot(slot_half, spread)
    wide = jnp.where(iota((16, 256), 0) == (iota((16, 256), 1) & 3), wide, 0.0)
    wide = jnp.sum(wide, axis=0, keepdims=True).astype(jnp.int32)
    back = onehot(iota((MOSTE, 256), 0) == wide)
    slot_weight = jnp.zeros((MOSTE, 1), F32)
    slot_whole = slot.astype(jnp.int32)
    for t in range(4):
        mine = iota((MOSTE, 64), 0) == slot_whole[t:t + 1]
        slot_weight = slot_weight + jnp.sum(
            jnp.where(mine, weights[t], 0.0), axis=1, keepdims=True
        )
    row, col = iota((WIDE, WIDE), 0), iota((WIDE, WIDE), 1)
    shift_ref[...] = onehot(
        ((row < SLICE) & (col == row))
        | ((row >= LANES) & (row < LANES + SLICE + 2) & (col == row - (LANES - SLICE)))
    )

    padn[...] = jnp.zeros((16, 128), F32)
    padn[0:4, :] = new_ref[...].astype(F32)
    fresh = padn[...].astype(BF16)
    loads[0].wait()
    live = iota((16, 128), 1) < len_ref[0]
    gen_s = jnp.where(live, dot(own, gen_ref[...], ((1,), (1,))), -1e30)
    causal = iota((16, 16), 1) <= (iota((16, 16), 0) & 3)
    new_s = jnp.where(causal, dot(own, fresh, ((1,), (1,))), -1e30)
    top = jnp.maximum(
        jnp.max(gen_s, axis=1, keepdims=True), jnp.max(new_s, axis=1, keepdims=True)
    )
    gen_w = jnp.exp(gen_s - top)
    new_w = jnp.exp(new_s - top)
    own_part = packed(
        top,
        jnp.sum(gen_w, axis=1, keepdims=True) + jnp.sum(new_w, axis=1, keepdims=True),
        dot(gen_w.astype(BF16), gen_ref[...]) + dot(new_w.astype(BF16), fresh),
    )
    padr[...] = jnp.zeros((8, LANES), F32)
    padr[0:4, 0:SLICE] = res_ref[...].astype(F32)
    padg[...] = jnp.zeros((1, LANES), F32)
    padg[:, 0:SLICE] = gain_ref[...]
    pl.semaphore_wait(barrier, len(partners))

    def attend(h):
        for cc in range(NC):
            for xx in range(NX):
                keys = prompt_ref[xx]
                s = dot(qbuf[h, cc, xx].reshape(64, 128), keys, ((1,), (1,)))
                m = jnp.max(s, axis=1, keepdims=True)
                w = jnp.exp(s - m)
                l = jnp.sum(w, axis=1, keepdims=True)
                part[h, cc, xx] = packed(m, l, dot(w.astype(BF16), keys)).reshape(NY, 16, 128)

    def share_y(h):
        return [start(qbuf.at[h, c, x, y], qbuf.at[h, c, x, y], device) for device in to_y]

    def share_x(h):
        return [start(qbuf.at[h, c, x], qbuf.at[h, c, x], device) for device in to_x]

    def share_core(h):
        return [start(qbuf.at[h, c], qbuf.at[h, c], to_core)]

    def sum_core(i, h):
        return [start(part.at[h, 1 - c], rc.at[i], to_core)]

    def add_core(i, h):
        rows = (NX * NY * 16, 128)
        s1[i] = merge([part[h, c].reshape(rows), rc[i].reshape(rows)]).reshape(s1.shape[1:])

    def sum_x(i):
        return [
            start(s1.at[i, lax.rem(x + d, NX)], rx.at[i, d - 1], to_x[d - 1])
            for d in range(1, NX)
        ]

    def add_x(i):
        rows = (NY * 16, 128)
        s2[i] = merge(
            [s1[i, x].reshape(rows)] + [rx[i, d].reshape(rows) for d in range(NX - 1)]
        ).reshape(s2.shape[1:])

    def sum_y(i):
        return [
            start(s2.at[i, lax.rem(y + d, NY)], ry.at[i, d - 1], to_y[d - 1])
            for d in range(1, NY)
        ]

    def add_y(i):
        s3[i] = merge([s2[i, y]] + [ry[i, d] for d in range(NY - 1)])

    far = 1 - z
    across = [start(qbuf.at[z, c, x, y], qbuf.at[z, c, x, y], to_z)]
    finish(share_y(z))
    finish(share_x(z))
    finish(share_core(z))
    loads[1].wait()
    attend(z)
    part[z, c, x, y] = merge([part[z, c, x, y], own_part])
    near = sum_core(0, z)
    finish(across)
    flight = share_y(far)
    finish(near)
    add_core(0, z)
    near = sum_x(0)
    finish(flight)
    flight = share_x(far)
    finish(near)
    add_x(0)
    near = sum_y(0)
    finish(flight)
    flight = share_core(far)
    finish(near)
    add_y(0)
    finish(flight)
    attend(far)
    finish(sum_core(1, far))
    add_core(1, far)
    finish(sum_x(1))
    add_x(1)
    finish(sum_y(1))
    add_y(1)
    finish([start(s3.at[1], rz, to_z)])
    final = merge([s3[0], rz[...]])
    lane = iota((16, 128), 1)
    attended = jnp.where(lane >= HEAD, final / final[:, 1:2], 0.0).astype(BF16)

    row, col = iota((128, 256), 0), iota((128, 256), 1)
    copies = onehot((row >= HEAD) & ((col & (HEAD - 1)) == row - HEAD))
    heads = jnp.where(own_head, dot(attended, copies), 0.0)
    steps = onehot((iota((16, 16), 1) & 3) == iota((16, 16), 0))
    attended = dot(steps, heads.astype(BF16)).astype(BF16)
    proj[:, PADDED - 128:] = jnp.zeros((8, 128), F32)
    loads[2].wait()
    proj[:, :D] = dot(attended, wout_ref[...], ((1,), (1,)))[0:8]
    for k in range(KV):
        rsend[k] = window(proj, k)[0:4].astype(BF16)
    finish([
        start(rsend.at[lax.rem(kv + d, KV)], rrecv.at[d - 1], to_kv[d - 1])
        for d in range(1, KV)
    ])
    projected = rsend[kv].astype(F32)
    for d in range(KV - 1):
        projected = projected + rrecv[d].astype(F32)
    lane = iota((4, LANES), 1)
    residual_sum = jnp.where(lane < SLICE, padr[0:4, :] + projected, 0.0)

    squares = jnp.sum(residual_sum * residual_sum, axis=1, keepdims=True)
    high = squares.astype(BF16).astype(F32)
    scaled = residual_sum * padg[...]
    agbuf[column] = jnp.where(
        lane == SLICE, high, jnp.where(lane == SLICE + 1, squares - high, scaled)
    ).astype(BF16)
    finish([start(agbuf.at[column], agbuf.at[column], device) for device in to_column])
    for zz in range(NZ):
        pieces = [agbuf[KV * zz + k].astype(F32) for k in range(KV)]
        squares = jnp.zeros((4, 1), F32)
        for piece in pieces:
            squares = squares + piece[:, SLICE:SLICE + 1] + piece[:, SLICE + 1:SLICE + 2]
        inverse = lax.rsqrt(squares / D + 1e-05)
        high = inverse.astype(BF16).astype(F32)
        for k, piece in enumerate(pieces):
            piece = jnp.where(
                lane == SLICE, high, jnp.where(lane == SLICE + 1, inverse - high, piece)
            )
            low, half = 16 * zz + 4 * (k // 2), LANES * (k % 2)
            blk[low:low + 4, half:half + LANES] = piece
    block = dot(blk[...].astype(BF16), shift_ref[...]).astype(BF16)
    ybuf[0, c, x, y] = block[0:16]
    ybuf[1, c, x, y] = block[16:32]

    a = [start(ybuf.at[0, c, x, y], ybuf.at[0, c, x, y], device) for device in to_y]
    b = [start(ybuf.at[1, c, x, y], ybuf.at[1, c, x, y], device) for device in to_x]
    finish(a)
    a = [start(ybuf.at[0, c, x], ybuf.at[0, c, x], device) for device in to_x]
    finish(b)
    b = [start(ybuf.at[1, c, :, y], ybuf.at[1, c, :, y], device) for device in to_y]
    finish(a)
    a = [start(ybuf.at[0, c], ybuf.at[0, c], to_core)]
    finish(b)
    b = [start(ybuf.at[1, c], ybuf.at[1, c], to_core)]
    for load in loads[3:]:
        load.wait()
    finish(a)
    finish(b)

    rows = dot(choose[...], ybuf[...].reshape(1024, WIDE))
    factor = rows[0:MOSTE, QUARTER:QUARTER + 1] + rows[0:MOSTE, QUARTER + 1:QUARTER + 2]
    xs[...] = jnp.zeros(xs.shape, F32)
    for j in range(4):
        low = QUARTER * j // 128 * 128
        features = jnp.where(
            iota((MOSTE, WIDE), 1) < QUARTER, rows[MOSTE * j:MOSTE * (j + 1)], 0.0
        )
        features = jnp.concatenate([features, jnp.zeros((MOSTE, 128), F32)], axis=1)
        if QUARTER * j - low:
            features = pltpu.roll(features, QUARTER * j - low, 1)
        xs[:, low:low + WIDE + 128] += features
    features = xs[:, :D].astype(BF16)
    gate = dot(features, wg_ref[...], ((1,), (1,))) * factor
    up = dot(features, wu_ref[...], ((1,), (1,))) * factor
    activation = (gate * jax.nn.sigmoid(1.702 * gate) * (up + 1.0)).astype(BF16)
    oflat[:, PADDED - 128:] = jnp.zeros((MOSTE, 128), F32)
    oflat[:, :D] = dot(activation, wd_ref[...]) * slot_weight
    for k in range(KV):
        esend[k] = window(oflat, k).astype(BF16)
    finish([
        start(esend.at[lax.rem(kv + d, KV)], erecv.at[d - 1], to_kv[d - 1])
        for d in range(1, KV)
    ])
    summed = esend[kv].astype(F32)
    for d in range(KV - 1):
        summed = summed + erecv[d].astype(F32)

    dense = dot(back, summed.astype(BF16), ((0,), (0,)))
    dn[...] = dense.astype(BF16).reshape(dn.shape)

    def fold_half(i, h):
        finish([start(dn.at[h, 1 - c], r1.at[i], to_core)])
        e1[i] = (dn[h, c].astype(F32) + r1[i].astype(F32)).reshape(NX, 16, LANES)
        finish([
            start(e1.at[i, lax.rem(x + d, NX)], rx2.at[i, d - 1], to_x[d - 1])
            for d in range(1, NX)
        ])
        total = e1[i, x] + rx2[i, 0] + rx2[i, 1] + rx2[i, 2]
        for yy in range(NY):
            e2[i, yy] = total[4 * yy:4 * yy + 4]
        finish([
            start(e2.at[i, lax.rem(y + d, NY)], ry2.at[i, d - 1], to_y[d - 1])
            for d in range(1, NY)
        ])
        e3[i] = e2[i, y] + ry2[i, 0] + ry2[i, 1] + ry2[i, 2]

    fold_half(1, far)
    across = [start(e3.at[1], rz2, to_z)]
    fold_half(0, z)
    finish(across)
    out = residual_sum + e3[0] + rz2[...]
    out_ref[...] = out[:, 0:SLICE].astype(BF16)


def on_device(
    queries, prompt_cache, gen_cache, gen_lengths, new_kv, w_out, residual, norm_gain,
    w_gate, w_up, w_down, expert_ids, route_weights,
):
    ffe = w_gate.shape[2]
    anywhere = pl.BlockSpec(memory_space=pl.ANY)
    vmem = pl.BlockSpec(memory_space=pltpu.VMEM)
    smem = pl.BlockSpec(memory_space=pltpu.SMEM)
    grid = (NZ, NC, NX, NY)
    scratch = [
        pltpu.VMEM(prompt_cache.shape, BF16),
        pltpu.VMEM(gen_cache.shape[1:], BF16),
        pltpu.VMEM((D, 256), BF16),
        pltpu.VMEM((ffe, D), BF16),
        pltpu.VMEM((ffe, D), BF16),
        pltpu.VMEM((ffe, D), BF16),
        pltpu.VMEM((16, 256), F32),
        pltpu.VMEM((16, 128), F32),
        pltpu.VMEM((8, LANES), F32),
        pltpu.VMEM((1, LANES), F32),
        pltpu.VMEM((16, 64), F32),
        pltpu.VMEM(grid + (16, 128), BF16),
        pltpu.VMEM(grid + (16, 128), F32),
        pltpu.VMEM((2, NX, NY, 16, 128), F32),
        pltpu.VMEM((2, NX, NY, 16, 128), F32),
        pltpu.VMEM((2, NX - 1, NY, 16, 128), F32),
        pltpu.VMEM((2, NY, 16, 128), F32),
        pltpu.VMEM((2, NY - 1, 16, 128), F32),
        pltpu.VMEM((2, 16, 128), F32),
        pltpu.VMEM((16, 128), F32),
        pltpu.VMEM((8, PADDED), F32),
        pltpu.VMEM((KV, 4, LANES), BF16),
        pltpu.VMEM((KV - 1, 4, LANES), BF16),
        pltpu.VMEM((NZ * KV, 4, LANES), BF16),
        pltpu.VMEM((32, WIDE), F32),
        pltpu.VMEM(grid + (16, WIDE), BF16),
        pltpu.VMEM((4 * MOSTE, 1024), BF16),
        pltpu.VMEM((WIDE, WIDE), BF16),
        pltpu.VMEM((MOSTE, PADDED), F32),
        pltpu.VMEM((MOSTE, PADDED), F32),
        pltpu.VMEM((KV, MOSTE, LANES), BF16),
        pltpu.VMEM((KV - 1, MOSTE, LANES), BF16),
        pltpu.VMEM((NZ, NC, 64, LANES), BF16),
        pltpu.VMEM((2, 64, LANES), BF16),
        pltpu.VMEM((2, NX, 16, LANES), F32),
        pltpu.VMEM((2, NX - 1, 16, LANES), F32),
        pltpu.VMEM((2, NY, 4, LANES), F32),
        pltpu.VMEM((2, NY - 1, 4, LANES), F32),
        pltpu.VMEM((2, 4, LANES), F32),
        pltpu.VMEM((4, LANES), F32),
        pltpu.SemaphoreType.DMA((96,)),
        pltpu.SemaphoreType.DMA((96,)),
        pltpu.SemaphoreType.DMA((6,)),
    ]
    out = pl.pallas_call(
        kernel,
        out_shape=jax.ShapeDtypeStruct(residual.shape[1:], BF16),
        in_specs=[vmem, anywhere, anywhere, vmem, smem, anywhere, vmem, vmem]
        + [anywhere] * 3 + [vmem] * 2,
        out_specs=vmem,
        scratch_shapes=scratch,
        compiler_params=pltpu.CompilerParams(
            collective_id=0, has_side_effects=True, vmem_limit_bytes=60 * 1024 * 1024
        ),
        name="layer",
    )(
        queries[0], prompt_cache, gen_cache[0], new_kv[0], gen_lengths, w_out.T, residual[0],
        norm_gain.reshape(1, SLICE), w_gate[0].T, w_up[0].T, w_down[0],
        expert_ids.transpose(1, 2, 0), route_weights.transpose(1, 2, 0),
    )
    return out[None]


def solution(mesh):
    in_specs = (
        P("roll", None, "kv"),
        P(None, "roll", "kv"),
        P("roll", None, "kv"),
        P("roll"),
        P("roll", None, "kv"),
        P("kv", None),
        P("roll", None, "kv"),
        P("kv"),
        P("roll", None, "kv"),
        P("roll", None, "kv"),
        P("roll", "kv", None),
        P(),
        P(),
    )
    out_specs = P("roll", None, "kv")
    return jax.shard_map(
        on_device, mesh=mesh, in_specs=in_specs, out_specs=out_specs, check_vma=False
    )
```

time: 137 us -> 119 us (0.87)
  the two profiles are of different devices: /device:TPU:64 before, /device:TPU:1 now
where the time goes in v2:
time: 119 us; the launch traced here: 117 us
  Pallas kernels  114 us (96%)
  local copies, waits for them, and re-layouts  2.51 us (2%)
    pallas_call x1, Pallas kernels, on_device(): pl.pallas_call(kernel, out_shape=jax.ShapeDtypeStruct(residual.shape[1:],...  114 us

profile of v2, /device:TPU:1, one launch (start us, length us, event | category | flops | bytes accessed | tf_op | source)
XLA Modules:
  0.0 117.0 jit_solution(6510879447493598983)
XLA Ops:
  0.7 1.2 %reshape.3.gain_ref = f32[1,360]{1,0:T(1,128)} reshape(f32[360]{0:T(512)} %param.20) | data formatting | bytes 2880 | tf_op jit(solution)/shard_map/reshape | solution.py:463
  1.9 113.8 %layer.1 = bf16[4,360]{1,0:T(4,128)(2,1)} custom-call(bf16[4,256]{1,0:T(4,128)(2,1)} %bitcast.24, bf16[4,256,128]{2,1,0:T(8,128)(2,1)} %prompt_hbm.1, bf16[128,128]{1,0:T(8,128)(2,1)} %bitcast.19, bf16[4,128]{1,0:T(4,128)(2,1)} %bitcast.25, s32[1]{0:T(128)S(6)} %copy.15.len_ref, bf16[2880,256]{1,0:T(8,128)(2,1)} %bitcast.15, bf16[4,360]{1,0:T(4,128)(2,1)} %bitcast.23, ...), custom_call_target="tpu_custom_call" | custom-call | tf_op jit(solution)/shard_map/layer/pallas_call | solution.py:450
  115.7 1.3 %copy.16 = bf16[1,4,360]{2,1,0:T(4,128)(2,1)} copy(bf16[1,4,360]{2,1,0:T(4,128)(2,1)} %bitcast.20) | data formatting | bytes 5760

commit v3 on v2

--- a/solution.py
+++ b/solution.py
@@ -62,7 +62,7 @@
     prompt_ref, gen_ref, wout_ref, wg_ref, wu_ref, wd_ref,
     padq, padn, padr, padg, pres,
     qbuf, part, rc, s1, rx, s2, ry, s3, rz,
-    proj, rsend, rrecv, agbuf, blk, ybuf, choose, shift_ref, xs,
+    proj, rsend, rrecv, agbuf, blk, ybuf, choose, xs,
     oflat, esend, erecv, dn, r1, e1, rx2, e2, ry2, e3, rz2,
     send_sem, recv_sem, load_sem,
 ):
@@ -147,6 +147,115 @@
             | ((sample >> 4) << 2) | ((sample >> 1) & 3)
         )
 
+    padr[...] = jnp.zeros((8, LANES), F32)
+    padr[0:4, 0:SLICE] = res_ref[...].astype(F32)
+    padg[...] = jnp.zeros((1, LANES), F32)
+    padg[:, 0:SLICE] = gain_ref[...]
+    pl.semaphore_wait(barrier, len(partners))
+
+    def attend(h):
+        scores = []
+        for xx in range(NX):
+            q = jnp.concatenate([qbuf[h, cc, xx].reshape(64, 128) for cc in range(NC)], axis=0)
+            scores.append(dot(q, prompt_ref[xx], ((1,), (1,))))
+        tops = [jnp.max(s, axis=1, keepdims=True) for s in scores]
+        scores = [jnp.exp(s - m) for s, m in zip(scores, tops)]
+        totals = [jnp.sum(w, axis=1, keepdims=True) for w in scores]
+        for xx in range(NX):
+            values = dot(scores[xx].astype(BF16), prompt_ref[xx])
+            rows = packed(tops[xx], totals[xx], values)
+            for cc in range(NC):
+                part[h, cc, xx] = rows[64 * cc:64 * (cc + 1)].reshape(NY, 16, 128)
+
+    def share_y(h):
+        return [start(qbuf.at[h, c, x, y], qbuf.at[h, c, x, y], device) for device in to_y]
+
+    def share_x(h):
+        return [start(qbuf.at[h, c, x], qbuf.at[h, c, x], device) for device in to_x]
+
+    def share_core(h):
+        return [start(qbuf.at[h, c], qbuf.at[h, c], to_core)]
+
+    def sum_core(i, h):
+        return [start(part.at[h, 1 - c], rc.at[i], to_core)]
+
+    def add_core(i, h):
+        rows = (NX * NY * 16, 128)
+        s1[i] = merge([part[h, c].reshape(rows), rc[i].reshape(rows)]).reshape(s1.shape[1:])
+
+    def sum_x(i):
+        return [
+            start(s1.at[i, lax.rem(x + d, NX)], rx.at[i, d - 1], to_x[d - 1])
+            for d in range(1, NX)
+        ]
+
+    def add_x(i):
+        rows = (NY * 16, 128)
+        s2[i] = merge(
+            [s1[i, x].reshape(rows)] + [rx[i, d].reshape(rows) for d in range(NX - 1)]
+        ).reshape(s2.shape[1:])
+
+    def sum_y(i):
+        return [
+            start(s2.at[i, lax.rem(y + d, NY)], ry.at[i, d - 1], to_y[d - 1])
+            for d in range(1, NY)
+        ]
+
+    def add_y(i):
+        s3[i] = merge([s2[i, y]] + [ry[i, d] for d in range(NY - 1)])
+
+    far = 1 - z
+    across = [start(qbuf.at[z, c, x, y], qbuf.at[z, c, x, y], to_z)]
+    flight = share_y(z)
+    padn[...] = jnp.zeros((16, 128), F32)
+    padn[0:4, :] = new_ref[...].astype(F32)
+    fresh = padn[...].astype(BF16)
+    loads[0].wait()
+    live = iota((16, 128), 1) < len_ref[0]
+    gen_s = jnp.where(live, dot(own, gen_ref[...], ((1,), (1,))), -1e30)
+    causal = iota((16, 16), 1) <= (iota((16, 16), 0) & 3)
+    new_s = jnp.where(causal, dot(own, fresh, ((1,), (1,))), -1e30)
+    top = jnp.maximum(
+        jnp.max(gen_s, axis=1, keepdims=True), jnp.max(new_s, axis=1, keepdims=True)
+    )
+    gen_w = jnp.exp(gen_s - top)
+    new_w = jnp.exp(new_s - top)
+    own_part = packed(
+        top,
+        jnp.sum(gen_w, axis=1, keepdims=True) + jnp.sum(new_w, axis=1, keepdims=True),
+        dot(gen_w.astype(BF16), gen_ref[...]) + dot(new_w.astype(BF16), fresh),
+    )
+    finish(flight)
+    finish(share_x(z))
+    finish(share_core(z))
+    finish(across)
+    flight = share_y(far)
+    loads[1].wait()
+    attend(z)
+    part[z, c, x, y] = merge([part[z, c, x, y], own_part])
+    near = sum_core(0, z)
+    finish(flight)
+    flight = share_x(far)
+    finish(near)
+    add_core(0, z)
+    near = sum_x(0)
+    finish(flight)
+    flight = share_core(far)
+    finish(near)
+    add_x(0)
+    near = sum_y(0)
+    finish(flight)
+    attend(far)
+    flight = sum_core(1, far)
+    finish(near)
+    add_y(0)
+    finish(flight)
+    add_core(1, far)
+    finish(sum_x(1))
+    add_x(1)
+    finish(sum_y(1))
+    add_y(1)
+    flight = [start(s3.at[1], rz, to_z)]
     spread = onehot(place(iota((64, 1024), 0)) == (iota((64, 1024), 1) >> 4))
     wide = dot(slot_half, spread)
     wide = jnp.where(iota((16, 1024), 0) == (iota((16, 1024), 1) & 3), wide, 0.0)
@@ -166,115 +275,7 @@
         slot_weight = slot_weight + jnp.sum(
             jnp.where(mine, weights[t], 0.0), axis=1, keepdims=True
         )
-    row, col = iota((WIDE, WIDE), 0), iota((WIDE, WIDE), 1)
-    shift_ref[...] = onehot(
-        ((row < SLICE) & (col == row))
-        | ((row >= LANES) & (row < LANES + SLICE + 2) & (col == row - (LANES - SLICE)))
-    )
-
-    padn[...] = jnp.zeros((16, 128), F32)
-    padn[0:4, :] = new_ref[...].astype(F32)
-    fresh = padn[...].astype(BF16)
-    loads[0].wait()
-    live = iota((16, 128), 1) < len_ref[0]
-    gen_s = jnp.where(live, dot(own, gen_ref[...], ((1,), (1,))), -1e30)
-    causal = iota((16, 16), 1) <= (iota((16, 16), 0) & 3)
-    new_s = jnp.where(causal, dot(own, fresh, ((1,), (1,))), -1e30)
-    top = jnp.maximum(
-        jnp.max(gen_s, axis=1, keepdims=True), jnp.max(new_s, axis=1, keepdims=True)
-    )
-    gen_w = jnp.exp(gen_s - top)
-    new_w = jnp.exp(new_s - top)
-    own_part = packed(
-        top,
-        jnp.sum(gen_w, axis=1, keepdims=True) + jnp.sum(new_w, axis=1, keepdims=True),
-        dot(gen_w.astype(BF16), gen_ref[...]) + dot(new_w.astype(BF16), fresh),
-    )
-    padr[...] = jnp.zeros((8, LANES), F32)
-    padr[0:4, 0:SLICE] = res_ref[...].astype(F32)
-    padg[...] = jnp.zeros((1, LANES), F32)
-    padg[:, 0:SLICE] = gain_ref[...]
-    pl.semaphore_wait(barrier, len(partners))
-
-    def attend(h):
-        for cc in range(NC):
-            for xx in range(NX):
-                keys = prompt_ref[xx]
-                s = dot(qbuf[h, cc, xx].reshape(64, 128), keys, ((1,), (1,)))
-                m = jnp.max(s, axis=1, keepdims=True)
-                w = jnp.exp(s - m)
-                l = jnp.sum(w, axis=1, keepdims=True)
-                part[h, cc, xx] = packed(m, l, dot(w.astype(BF16), keys)).reshape(NY, 16, 128)
-
-    def share_y(h):
-        return [start(qbuf.at[h, c, x, y], qbuf.at[h, c, x, y], device) for device in to_y]
-
-    def share_x(h):
-        return [start(qbuf.at[h, c, x], qbuf.at[h, c, x], device) for device in to_x]
-
-    def share_core(h):
-        return [start(qbuf.at[h, c], qbuf.at[h, c], to_core)]
-
-    def sum_core(i, h):
-        return [start(part.at[h, 1 - c], rc.at[i], to_core)]
-
-    def add_core(i, h):
-        rows = (NX * NY * 16, 128)
-        s1[i] = merge([part[h, c].reshape(rows), rc[i].reshape(rows)]).reshape(s1.shape[1:])
-
-    def sum_x(i):
-        return [
-            start(s1.at[i, lax.rem(x + d, NX)], rx.at[i, d - 1], to_x[d - 1])
-            for d in range(1, NX)
-        ]
-
-    def add_x(i):
-        rows = (NY * 16, 128)
-        s2[i] = merge(
-            [s1[i, x].reshape(rows)] + [rx[i, d].reshape(rows) for d in range(NX - 1)]
-        ).reshape(s2.shape[1:])
-
-    def sum_y(i):
-        return [
-            start(s2.at[i, lax.rem(y + d, NY)], ry.at[i, d - 1], to_y[d - 1])
-            for d in range(1, NY)
-        ]
-
-    def add_y(i):
-        s3[i] = merge([s2[i, y]] + [ry[i, d] for d in range(NY - 1)])
-
-    far = 1 - z
-    across = [start(qbuf.at[z, c, x, y], qbuf.at[z, c, x, y], to_z)]
-    finish(share_y(z))
-    finish(share_x(z))
-    finish(share_core(z))
-    loads[1].wait()
-    attend(z)
-    part[z, c, x, y] = merge([part[z, c, x, y], own_part])
-    near = sum_core(0, z)
-    finish(across)
-    flight = share_y(far)
-    finish(near)
-    add_core(0, z)
-    near = sum_x(0)
-    finish(flight)
-    flight = share_x(far)
-    finish(near)
-    add_x(0)
-    near = sum_y(0)
-    finish(flight)
-    flight = share_core(far)
-    finish(near)
-    add_y(0)
-    finish(flight)
-    attend(far)
-    finish(sum_core(1, far))
-    add_core(1, far)
-    finish(sum_x(1))
-    add_x(1)
-    finish(sum_y(1))
-    add_y(1)
-    finish([start(s3.at[1], rz, to_z)])
+    finish(flight)
     final = merge([s3[0], rz[...]])
     lane = iota((16, 128), 1)
     attended = jnp.where(lane >= HEAD, final / final[:, 1:2], 0.0).astype(BF16)
@@ -319,7 +320,10 @@
             )
             low, half = 16 * zz + 4 * (k // 2), LANES * (k % 2)
             blk[low:low + 4, half:half + LANES] = piece
-    block = dot(blk[...].astype(BF16), shift_ref[...]).astype(BF16)
+    block = blk[...]
+    block = jnp.where(
+        iota(block.shape, 1) < SLICE, block, pltpu.roll(block, WIDE - (LANES - SLICE), 1)
+    ).astype(BF16)
     ybuf[0, c, x, y] = block[0:16]
     ybuf[1, c, x, y] = block[16:32]
 
@@ -430,7 +434,6 @@
         pltpu.VMEM((32, WIDE), F32),
         pltpu.VMEM(grid + (16, WIDE), BF16),
         pltpu.VMEM((4 * MOSTE, 1024), BF16),
-        pltpu.VMEM((WIDE, WIDE), BF16),
         pltpu.VMEM((MOSTE, PADDED), F32),
         pltpu.VMEM((MOSTE, PADDED), F32),
         pltpu.VMEM((KV, MOSTE, LANES), BF16),

time: 119 us -> 115 us (0.966)
  Pallas kernels: 114 us -> 110 us
    pallas_call x1, Pallas kernels: 114 us -> 110 us  [on_device(): pl.pallas_call(kernel, out_shape=jax.ShapeDtypeStruct(residual.shape[1:],...]
where the time goes in v3:
time: 115 us; the launch traced here: 113 us
  Pallas kernels  110 us (96%)
  local copies, waits for them, and re-layouts  2.51 us (2%)
    pallas_call x1, Pallas kernels, on_device(): pl.pallas_call(kernel, out_shape=jax.ShapeDtypeStruct(residual.shape[1:],...  110 us

profile of v3, /device:TPU:1, one launch (start us, length us, event | category | flops | bytes accessed | tf_op | source)
XLA Modules:
  0.0 113.1 jit_solution(1926622514882948196)
XLA Ops:
  0.7 1.2 %reshape.3.gain_ref = f32[1,360]{1,0:T(1,128)} reshape(f32[360]{0:T(512)} %param.20) | data formatting | bytes 2880 | tf_op jit(solution)/shard_map/reshape | solution.py:466
  1.9 109.9 %layer.1 = bf16[4,360]{1,0:T(4,128)(2,1)} custom-call(bf16[4,256]{1,0:T(4,128)(2,1)} %bitcast.24, bf16[4,256,128]{2,1,0:T(8,128)(2,1)} %prompt_hbm.1, bf16[128,128]{1,0:T(8,128)(2,1)} %bitcast.19, bf16[4,128]{1,0:T(4,128)(2,1)} %bitcast.25, s32[1]{0:T(128)S(6)} %copy.15.len_ref, bf16[2880,256]{1,0:T(8,128)(2,1)} %bitcast.15, bf16[4,360]{1,0:T(4,128)(2,1)} %bitcast.23, ...), custom_call_target="tpu_custom_call" | custom-call | tf_op jit(solution)/shard_map/layer/pallas_call | solution.py:453
  111.8 1.3 %copy.16 = bf16[1,4,360]{2,1,0:T(4,128)(2,1)} copy(bf16[1,4,360]{2,1,0:T(4,128)(2,1)} %bitcast.20) | data formatting | bytes 5760

commit v4 on v3

--- a/solution.py
+++ b/solution.py
@@ -61,9 +61,9 @@
     wg_hbm, wu_hbm, wd_hbm, ids_ref, rw_ref, out_ref,
     prompt_ref, gen_ref, wout_ref, wg_ref, wu_ref, wd_ref,
     padq, padn, padr, padg, pres,
-    qbuf, part, rc, s1, rx, s2, ry, s3, rz,
+    qbuf, part, rc, s1, rx, s3, rz,
     proj, rsend, rrecv, agbuf, blk, ybuf, choose, xs,
-    oflat, esend, erecv, dn, r1, e1, rx2, e2, ry2, e3, rz2,
+    oflat, esend, erecv, dn, r1, e1, rx2, e3, rz2,
     send_sem, recv_sem, load_sem,
 ):
     roll = lax.axis_index("roll")
@@ -80,13 +80,16 @@
     to_z = at(x, 1 - z, y, c)
     to_x = [at(lax.rem(x + d, NX), z, y, c) for d in range(1, NX)]
     to_y = [at(x, z, lax.rem(y + d, NY), c) for d in range(1, NY)]
+    others = [(dx, dy) for dx in range(NX) for dy in range(NY) if dx or dy]
+    in_plane = [(lax.rem(x + dx, NX), lax.rem(y + dy, NY)) for dx, dy in others]
+    to_plane = [at(xx, z, yy, c) for xx, yy in in_plane]
     to_kv = [(roll, lax.rem(kv + d, KV)) for d in range(1, KV)]
     column = z * KV + kv
     to_column = []
     for d in range(1, NZ * KV):
         there = lax.rem(column + d, NZ * KV)
         to_column.append((at(x, there // KV, y, c)[0], lax.rem(there, KV)))
-    partners = [to_core] + to_x + to_y + to_column
+    partners = [to_core] + to_plane + to_column
     barrier = pltpu.get_barrier_semaphore()
     for device in partners:
         pl.semaphore_signal(barrier, inc=1, device_id=device, device_id_type=MESH)
@@ -167,11 +170,8 @@
             for cc in range(NC):
                 part[h, cc, xx] = rows[64 * cc:64 * (cc + 1)].reshape(NY, 16, 128)
 
-    def share_y(h):
-        return [start(qbuf.at[h, c, x, y], qbuf.at[h, c, x, y], device) for device in to_y]
-
-    def share_x(h):
-        return [start(qbuf.at[h, c, x], qbuf.at[h, c, x], device) for device in to_x]
+    def share_plane(h):
+        return [start(qbuf.at[h, c, x, y], qbuf.at[h, c, x, y], device) for device in to_plane]
 
     def share_core(h):
         return [start(qbuf.at[h, c], qbuf.at[h, c], to_core)]
@@ -183,30 +183,18 @@
         rows = (NX * NY * 16, 128)
         s1[i] = merge([part[h, c].reshape(rows), rc[i].reshape(rows)]).reshape(s1.shape[1:])
 
-    def sum_x(i):
+    def sum_plane(i):
         return [
-            start(s1.at[i, lax.rem(x + d, NX)], rx.at[i, d - 1], to_x[d - 1])
-            for d in range(1, NX)
+            start(s1.at[i, xx, yy], rx.at[i, k], to_plane[k])
+            for k, (xx, yy) in enumerate(in_plane)
         ]
 
-    def add_x(i):
-        rows = (NY * 16, 128)
-        s2[i] = merge(
-            [s1[i, x].reshape(rows)] + [rx[i, d].reshape(rows) for d in range(NX - 1)]
-        ).reshape(s2.shape[1:])
-
-    def sum_y(i):
-        return [
-            start(s2.at[i, lax.rem(y + d, NY)], ry.at[i, d - 1], to_y[d - 1])
-            for d in range(1, NY)
-        ]
-
-    def add_y(i):
-        s3[i] = merge([s2[i, y]] + [ry[i, d] for d in range(NY - 1)])
+    def add_plane(i):
+        s3[i] = merge([s1[i, x, y]] + [rx[i, k] for k in range(len(others))])
 
     far = 1 - z
     across = [start(qbuf.at[z, c, x, y], qbuf.at[z, c, x, y], to_z)]
-    flight = share_y(z)
+    flight = share_plane(z)
     padn[...] = jnp.zeros((16, 128), F32)
     padn[0:4, :] = new_ref[...].astype(F32)
     fresh = padn[...].astype(BF16)
@@ -226,35 +214,27 @@
         dot(gen_w.astype(BF16), gen_ref[...]) + dot(new_w.astype(BF16), fresh),
     )
     finish(flight)
-    finish(share_x(z))
     finish(share_core(z))
     finish(across)
-    flight = share_y(far)
+    flight = share_plane(far)
     loads[1].wait()
     attend(z)
     part[z, c, x, y] = merge([part[z, c, x, y], own_part])
     near = sum_core(0, z)
     finish(flight)
-    flight = share_x(far)
+    flight = share_core(far)
     finish(near)
     add_core(0, z)
-    near = sum_x(0)
-    finish(flight)
-    flight = share_core(far)
-    finish(near)
-    add_x(0)
-    near = sum_y(0)
+    near = sum_plane(0)
     finish(flight)
     attend(far)
     flight = sum_core(1, far)
     finish(near)
-    add_y(0)
+    add_plane(0)
     finish(flight)
     add_core(1, far)
-    finish(sum_x(1))
-    add_x(1)
-    finish(sum_y(1))
-    add_y(1)
+    finish(sum_plane(1))
+    add_plane(1)
     flight = [start(s3.at[1], rz, to_z)]
     spread = onehot(place(iota((64, 1024), 0)) == (iota((64, 1024), 1) >> 4))
     wide = dot(slot_half, spread)
@@ -375,19 +355,19 @@
 
     def fold_half(i, h):
         finish([start(dn.at[h, 1 - c], r1.at[i], to_core)])
-        e1[i] = (dn[h, c].astype(F32) + r1[i].astype(F32)).reshape(NX, 16, LANES)
+        total = dn[h, c].astype(F32) + r1[i].astype(F32)
+        for xx in range(NX):
+            for yy in range(NY):
+                low = 4 * (NY * xx + yy)
+                e1[i, xx, yy] = total[low:low + 4]
         finish([
-            start(e1.at[i, lax.rem(x + d, NX)], rx2.at[i, d - 1], to_x[d - 1])
-            for d in range(1, NX)
+            start(e1.at[i, xx, yy], rx2.at[i, k], to_plane[k])
+            for k, (xx, yy) in enumerate(in_plane)
         ])
-        total = e1[i, x] + rx2[i, 0] + rx2[i, 1] + rx2[i, 2]
-        for yy in range(NY):
-            e2[i, yy] = total[4 * yy:4 * yy + 4]
-        finish([
-            start(e2.at[i, lax.rem(y + d, NY)], ry2.at[i, d - 1], to_y[d - 1])
-            for d in range(1, NY)
-        ])
-        e3[i] = e2[i, y] + ry2[i, 0] + ry2[i, 1] + ry2[i, 2]
+        total = e1[i, x, y]
+        for k in range(len(others)):
+            total = total + rx2[i, k]
+        e3[i] = total
 
     fold_half(1, far)
     across = [start(e3.at[1], rz2, to_z)]
@@ -422,9 +402,7 @@
         pltpu.VMEM(grid + (16, 128), F32),
         pltpu.VMEM((2, NX, NY, 16, 128), F32),
         pltpu.VMEM((2, NX, NY, 16, 128), F32),
-        pltpu.VMEM((2, NX - 1, NY, 16, 128), F32),
-        pltpu.VMEM((2, NY, 16, 128), F32),
-        pltpu.VMEM((2, NY - 1, 16, 128), F32),
+        pltpu.VMEM((2, NX * NY - 1, 16, 128), F32),
         pltpu.VMEM((2, 16, 128), F32),
         pltpu.VMEM((16, 128), F32),
         pltpu.VMEM((8, PADDED), F32),
@@ -440,14 +418,12 @@
         pltpu.VMEM((KV - 1, MOSTE, LANES), BF16),
         pltpu.VMEM((NZ, NC, 64, LANES), BF16),
         pltpu.VMEM((2, 64, LANES), BF16),
-        pltpu.VMEM((2, NX, 16, LANES), F32),
-        pltpu.VMEM((2, NX - 1, 16, LANES), F32),
-        pltpu.VMEM((2, NY, 4, LANES), F32),
-        pltpu.VMEM((2, NY - 1, 4, LANES), F32),
+        pltpu.VMEM((2, NX, NY, 4, LANES), F32),
+        pltpu.VMEM((2, NX * NY - 1, 4, LANES), F32),
         pltpu.VMEM((2, 4, LANES), F32),
         pltpu.VMEM((4, LANES), F32),
-        pltpu.SemaphoreType.DMA((96,)),
-        pltpu.SemaphoreType.DMA((96,)),
+        pltpu.SemaphoreType.DMA((160,)),
+        pltpu.SemaphoreType.DMA((160,)),
         pltpu.SemaphoreType.DMA((6,)),
     ]
     out = pl.pallas_call(

time: 115 us -> 108 us (0.939)
  the two profiles are of different devices: /device:TPU:1 before, /device:TPU:64 now
where the time goes in v4:
time: 108 us
  Pallas kernels  105 us (97%)
  local copies, waits for them, and re-layouts  2.51 us (2%)
    pallas_call x1, Pallas kernels, on_device(): pl.pallas_call(kernel, out_shape=jax.ShapeDtypeStruct(residual.shape[1:],...  105 us

profile of v4, /device:TPU:64, one launch (start us, length us, event | category | flops | bytes accessed | tf_op | source)
XLA Modules:
  0.0 108.1 jit_solution(15560552237192920891)
XLA Ops:
  0.7 1.2 %reshape.3.gain_ref = f32[1,360]{1,0:T(1,128)} reshape(f32[360]{0:T(512)} %param.20) | data formatting | bytes 2880 | tf_op jit(solution)/shard_map/reshape | solution.py:442
  1.9 105.0 %layer.1 = bf16[4,360]{1,0:T(4,128)(2,1)} custom-call(bf16[4,256]{1,0:T(4,128)(2,1)} %bitcast.24, bf16[4,256,128]{2,1,0:T(8,128)(2,1)} %prompt_hbm.1, bf16[128,128]{1,0:T(8,128)(2,1)} %bitcast.19, bf16[4,128]{1,0:T(4,128)(2,1)} %bitcast.25, s32[1]{0:T(128)S(6)} %copy.15.len_ref, bf16[2880,256]{1,0:T(8,128)(2,1)} %bitcast.15, bf16[4,360]{1,0:T(4,128)(2,1)} %bitcast.23, ...), custom_call_target="tpu_custom_call" | custom-call | tf_op jit(solution)/shard_map/layer/pallas_call | solution.py:429
  106.9 1.3 %copy.16 = bf16[1,4,360]{2,1,0:T(4,128)(2,1)} copy(bf16[1,4,360]{2,1,0:T(4,128)(2,1)} %bitcast.20) | data formatting | bytes 5760

commit v5 on v4

--- a/solution.py
+++ b/solution.py
@@ -81,12 +81,18 @@
     to_x = [at(lax.rem(x + d, NX), z, y, c) for d in range(1, NX)]
     to_y = [at(x, z, lax.rem(y + d, NY), c) for d in range(1, NY)]
     others = [(dx, dy) for dx in range(NX) for dy in range(NY) if dx or dy]
+    others.sort(key=lambda d: -min(d[0], NX - d[0]) - min(d[1], NY - d[1]))
     in_plane = [(lax.rem(x + dx, NX), lax.rem(y + dy, NY)) for dx, dy in others]
     to_plane = [at(xx, z, yy, c) for xx, yy in in_plane]
-    to_kv = [(roll, lax.rem(kv + d, KV)) for d in range(1, KV)]
+    bits = [lax.rem(kv, 2), lax.rem(kv // 2, 2), kv // 4]
+    peers = [
+        sum((1 - bit if m >> i & 1 else bit) * (1 << i) for i, bit in enumerate(bits))
+        for m in (7, 6, 5, 4, 3, 2, 1)
+    ]
+    to_kv = [(roll, peer) for peer in peers]
     column = z * KV + kv
     to_column = []
-    for d in range(1, NZ * KV):
+    for d in sorted(range(1, NZ * KV), key=lambda d: abs(d - KV)):
         there = lax.rem(column + d, NZ * KV)
         to_column.append((at(x, there // KV, y, c)[0], lax.rem(there, KV)))
     partners = [to_core] + to_plane + to_column
@@ -153,7 +159,7 @@
     padr[...] = jnp.zeros((8, LANES), F32)
     padr[0:4, 0:SLICE] = res_ref[...].astype(F32)
     padg[...] = jnp.zeros((1, LANES), F32)
-    padg[:, 0:SLICE] = gain_ref[...]
+    padg[:, 0:SLICE] = gain_ref[...].reshape(1, SLICE)
     pl.semaphore_wait(barrier, len(partners))
 
     def attend(h):
@@ -271,8 +277,7 @@
     for k in range(KV):
         rsend[k] = window(proj, k)[0:4].astype(BF16)
     finish([
-        start(rsend.at[lax.rem(kv + d, KV)], rrecv.at[d - 1], to_kv[d - 1])
-        for d in range(1, KV)
+        start(rsend.at[peer], rrecv.at[k], to_kv[k]) for k, peer in enumerate(peers)
     ])
     projected = rsend[kv].astype(F32)
     for d in range(KV - 1):
@@ -311,16 +316,20 @@
     b = [start(ybuf.at[1, c, x, y], ybuf.at[1, c, x, y], device) for device in to_x]
     finish(a)
     a = [start(ybuf.at[0, c, x], ybuf.at[0, c, x], device) for device in to_x]
+    cores = [start(ybuf.at[0, c, x], ybuf.at[0, c, x], to_core)]
     finish(b)
     b = [start(ybuf.at[1, c, :, y], ybuf.at[1, c, :, y], device) for device in to_y]
-    finish(a)
-    a = [start(ybuf.at[0, c], ybuf.at[0, c], to_core)]
-    finish(b)
-    b = [start(ybuf.at[1, c], ybuf.at[1, c], to_core)]
+    cores.append(start(ybuf.at[1, c, :, y], ybuf.at[1, c, :, y], to_core))
+    for d in (1, 3, 2):
+        a[d - 1].wait()
+        xx = lax.rem(x + NX - d, NX)
+        cores.append(start(ybuf.at[0, c, xx], ybuf.at[0, c, xx], to_core))
+        b[d - 1].wait()
+        yy = lax.rem(y + NY - d, NY)
+        cores.append(start(ybuf.at[1, c, :, yy], ybuf.at[1, c, :, yy], to_core))
     for load in loads[3:]:
         load.wait()
-    finish(a)
-    finish(b)
+    finish(cores)
 
     rows = dot(choose[...], ybuf[...].reshape(1024, WIDE))
     factor = rows[0:MOSTE, QUARTER:QUARTER + 1] + rows[0:MOSTE, QUARTER + 1:QUARTER + 2]
@@ -343,8 +352,7 @@
     for k in range(KV):
         esend[k] = window(oflat, k).astype(BF16)
     finish([
-        start(esend.at[lax.rem(kv + d, KV)], erecv.at[d - 1], to_kv[d - 1])
-        for d in range(1, KV)
+        start(esend.at[peer], erecv.at[k], to_kv[k]) for k, peer in enumerate(peers)
     ])
     summed = esend[kv].astype(F32)
     for d in range(KV - 1):
@@ -439,7 +447,7 @@
         name="layer",
     )(
         queries[0], prompt_cache, gen_cache[0], new_kv[0], gen_lengths, w_out.T, residual[0],
-        norm_gain.reshape(1, SLICE), w_gate[0].T, w_up[0].T, w_down[0],
+        norm_gain, w_gate[0].T, w_up[0].T, w_down[0],
         expert_ids.transpose(1, 2, 0), route_weights.transpose(1, 2, 0),
     )
     return out[None]

time: 108 us -> 107 us (level)
  the two profiles are of different devices: /device:TPU:64 before, /device:TPU:1 now
where the time goes in v5:
time: 107 us
  Pallas kernels  105 us (98%)
  local copies, waits for them, and re-layouts  1.26 us (1%)
    pallas_call x1, Pallas kernels, on_device(): pl.pallas_call(kernel, out_shape=jax.ShapeDtypeStruct(residual.shape[1:],...  105 us

profile of v5, /device:TPU:1, one launch (start us, length us, event | category | flops | bytes accessed | tf_op | source)
XLA Modules:
  0.0 106.9 jit_solution(8666995284517731161)
XLA Ops:
  0.7 105.0 %layer.1 = bf16[4,360]{1,0:T(4,128)(2,1)} custom-call(bf16[4,256]{1,0:T(4,128)(2,1)} %bitcast.24, bf16[4,256,128]{2,1,0:T(8,128)(2,1)} %prompt_hbm.1, bf16[128,128]{1,0:T(8,128)(2,1)} %bitcast.19, bf16[4,128]{1,0:T(4,128)(2,1)} %bitcast.25, s32[1]{0:T(128)S(6)} %copy.15.len_ref, bf16[2880,256]{1,0:T(8,128)(2,1)} %bitcast.15, bf16[4,360]{1,0:T(4,128)(2,1)} %bitcast.23, ...), custom_call_target="tpu_custom_call" | custom-call | tf_op jit(solution)/shard_map/layer/pallas_call | solution.py:437
  105.7 1.3 %copy.16 = bf16[1,4,360]{2,1,0:T(4,128)(2,1)} copy(bf16[1,4,360]{2,1,0:T(4,128)(2,1)} %bitcast.20) | data formatting | bytes 5760

commit v6 on v5

--- a/solution.py
+++ b/solution.py
@@ -34,17 +34,20 @@
 
 def packed(m, l, acc):
     lane = iota(acc.shape, 1)
-    return jnp.where(lane == 0, m, jnp.where(lane == 1, l, jnp.where(lane >= HEAD, acc, 0.0)))
+    high = l.astype(BF16).astype(F32)
+    acc = jnp.where(lane >= HEAD, acc, 0.0)
+    return jnp.where(lane == 0, m, jnp.where(lane == 1, high, jnp.where(lane == 2, l - high, acc)))
 
 
 def merge(rows):
+    rows = [r.astype(F32) for r in rows]
     top = rows[0][:, 0:1]
     for r in rows[1:]:
         top = jnp.maximum(top, r[:, 0:1])
     total = rows[0] * jnp.exp(rows[0][:, 0:1] - top)
     for r in rows[1:]:
         total = total + r * jnp.exp(r[:, 0:1] - top)
-    return jnp.where(iota(total.shape, 1) == 0, top, total)
+    return packed(top, total[:, 1:2] + total[:, 2:3], total)
 
 
 def window(ref, k):
@@ -167,12 +170,12 @@
         for xx in range(NX):
             q = jnp.concatenate([qbuf[h, cc, xx].reshape(64, 128) for cc in range(NC)], axis=0)
             scores.append(dot(q, prompt_ref[xx], ((1,), (1,))))
-        tops = [jnp.max(s, axis=1, keepdims=True) for s in scores]
+        tops = [jnp.max(s, axis=1, keepdims=True).astype(BF16).astype(F32) for s in scores]
         scores = [jnp.exp(s - m) for s, m in zip(scores, tops)]
         totals = [jnp.sum(w, axis=1, keepdims=True) for w in scores]
         for xx in range(NX):
             values = dot(scores[xx].astype(BF16), prompt_ref[xx])
-            rows = packed(tops[xx], totals[xx], values)
+            rows = packed(tops[xx], totals[xx], values).astype(BF16)
             for cc in range(NC):
                 part[h, cc, xx] = rows[64 * cc:64 * (cc + 1)].reshape(NY, 16, 128)
 
@@ -187,7 +190,8 @@
 
     def add_core(i, h):
         rows = (NX * NY * 16, 128)
-        s1[i] = merge([part[h, c].reshape(rows), rc[i].reshape(rows)]).reshape(s1.shape[1:])
+        total = merge([part[h, c].reshape(rows), rc[i].reshape(rows)])
+        s1[i] = total.astype(BF16).reshape(s1.shape[1:])
 
     def sum_plane(i):
         return [
@@ -211,7 +215,7 @@
     new_s = jnp.where(causal, dot(own, fresh, ((1,), (1,))), -1e30)
     top = jnp.maximum(
         jnp.max(gen_s, axis=1, keepdims=True), jnp.max(new_s, axis=1, keepdims=True)
-    )
+    ).astype(BF16).astype(F32)
     gen_w = jnp.exp(gen_s - top)
     new_w = jnp.exp(new_s - top)
     own_part = packed(
@@ -225,7 +229,7 @@
     flight = share_plane(far)
     loads[1].wait()
     attend(z)
-    part[z, c, x, y] = merge([part[z, c, x, y], own_part])
+    part[z, c, x, y] = merge([part[z, c, x, y], own_part]).astype(BF16)
     near = sum_core(0, z)
     finish(flight)
     flight = share_core(far)
@@ -264,7 +268,7 @@
     finish(flight)
     final = merge([s3[0], rz[...]])
     lane = iota((16, 128), 1)
-    attended = jnp.where(lane >= HEAD, final / final[:, 1:2], 0.0).astype(BF16)
+    attended = jnp.where(lane >= HEAD, final / (final[:, 1:2] + final[:, 2:3]), 0.0).astype(BF16)
 
     row, col = iota((128, 256), 0), iota((128, 256), 1)
     copies = onehot((row >= HEAD) & ((col & (HEAD - 1)) == row - HEAD))
@@ -367,14 +371,14 @@
         for xx in range(NX):
             for yy in range(NY):
                 low = 4 * (NY * xx + yy)
-                e1[i, xx, yy] = total[low:low + 4]
+                e1[i, xx, yy] = total[low:low + 4].astype(BF16)
         finish([
             start(e1.at[i, xx, yy], rx2.at[i, k], to_plane[k])
             for k, (xx, yy) in enumerate(in_plane)
         ])
-        total = e1[i, x, y]
+        total = e1[i, x, y].astype(F32)
         for k in range(len(others)):
-            total = total + rx2[i, k]
+            total = total + rx2[i, k].astype(F32)
         e3[i] = total
 
     fold_half(1, far)
@@ -407,10 +411,10 @@
         pltpu.VMEM((1, LANES), F32),
         pltpu.VMEM((16, 64), F32),
         pltpu.VMEM(grid + (16, 128), BF16),
-        pltpu.VMEM(grid + (16, 128), F32),
-        pltpu.VMEM((2, NX, NY, 16, 128), F32),
-        pltpu.VMEM((2, NX, NY, 16, 128), F32),
-        pltpu.VMEM((2, NX * NY - 1, 16, 128), F32),
+        pltpu.VMEM(grid + (16, 128), BF16),
+        pltpu.VMEM((2, NX, NY, 16, 128), BF16),
+        pltpu.VMEM((2, NX, NY, 16, 128), BF16),
+        pltpu.VMEM((2, NX * NY - 1, 16, 128), BF16),
         pltpu.VMEM((2, 16, 128), F32),
         pltpu.VMEM((16, 128), F32),
         pltpu.VMEM((8, PADDED), F32),
@@ -426,8 +430,8 @@
         pltpu.VMEM((KV - 1, MOSTE, LANES), BF16),
         pltpu.VMEM((NZ, NC, 64, LANES), BF16),
         pltpu.VMEM((2, 64, LANES), BF16),
-        pltpu.VMEM((2, NX, NY, 4, LANES), F32),
-        pltpu.VMEM((2, NX * NY - 1, 4, LANES), F32),
+        pltpu.VMEM((2, NX, NY, 4, LANES), BF16),
+        pltpu.VMEM((2, NX * NY - 1, 4, LANES), BF16),
         pltpu.VMEM((2, 4, LANES), F32),
         pltpu.VMEM((4, LANES), F32),
         pltpu.SemaphoreType.DMA((160,)),

time: 107 us -> 107 us (level)
  no operation moved by 1% of the time
where the time goes in v6:
time: 107 us
  Pallas kernels  105 us (98%)
  local copies, waits for them, and re-layouts  1.26 us (1%)
    pallas_call x1, Pallas kernels, on_device(): pl.pallas_call(kernel, out_shape=jax.ShapeDtypeStruct(residual.shape[1:],...  105 us

profile of v6, /device:TPU:1, one launch (start us, length us, event | category | flops | bytes accessed | tf_op | source)
XLA Modules:
  0.0 107.3 jit_solution(9273433422911717024)
XLA Ops:
  0.7 105.3 %layer.1 = bf16[4,360]{1,0:T(4,128)(2,1)} custom-call(bf16[4,256]{1,0:T(4,128)(2,1)} %bitcast.24, bf16[4,256,128]{2,1,0:T(8,128)(2,1)} %prompt_hbm.1, bf16[128,128]{1,0:T(8,128)(2,1)} %bitcast.19, bf16[4,128]{1,0:T(4,128)(2,1)} %bitcast.25, s32[1]{0:T(128)S(6)} %copy.15.len_ref, bf16[2880,256]{1,0:T(8,128)(2,1)} %bitcast.15, bf16[4,360]{1,0:T(4,128)(2,1)} %bitcast.23, ...), custom_call_target="tpu_custom_call" | custom-call | tf_op jit(solution)/shard_map/layer/pallas_call | solution.py:441
  106.0 1.3 %copy.16 = bf16[1,4,360]{2,1,0:T(4,128)(2,1)} copy(bf16[1,4,360]{2,1,0:T(4,128)(2,1)} %bitcast.20) | data formatting | bytes 5760
